TPU v7x, 512 devices: a whole 4x4x16 slice. The times are simulated.
512 devices in a mesh: layer: 8 (over y, core), latent: 64 (over x, z).
Axes of the slice: x: 4, y: 4, z: 16, core: 2. Of those that a mesh axis runs over, the one named last changes fastest.
Arguments:
- resid: bfloat16 [4, 128, 3584], P(None, 'latent'), may hold values from -6 to 6
- target: bfloat16 [5, 128, 3584], P(None, 'latent'), may hold values from -6 to 6
- enc_weight: bfloat16 [8, 3584, 8192], P('layer', None, 'latent'), may hold values from -0.09375 to 0.09375
- enc_bias: float32 [8, 8192], P('layer', 'latent'), may hold values from -3 to 3
- dec_weight: bfloat16 [8, 2, 2, 8192, 1792], P('layer', None, None, 'latent'), may hold values from -0.046875 to 0.046875
- blocks: int32 [4, 1, 96], replicated, may hold values from 0 to 127, all different within a row
Outputs:
- errors: bfloat16 [8, 128, 1792], P('layer', 'latent')
- enc_grad: bfloat16 [8, 3584, 8192], P('layer', None, 'latent')
- bias_grad: float32 [8, 8192], P('layer', 'latent')
Inputs may be any that keep to these rules, and one draw needn't show every extreme that they name: Each row names 96 different blocks; every block is named in some row.
All inputs are finite; a program needn't handle non-finite values.
Results may differ from a plain program's by a relative error of at most 0.007.
Values may be sent and summed in bfloat16 or wider, within the bound.
A program may use at most 64 MiB of HBM per device.

v0:
```python
import jax
import jax.numpy as jnp
from jax import lax
from jax.sharding import Mesh
from jax.sharding import PartitionSpec as P

LATENT = ("latent_0", "latent_1")


def laid_out(pieces, dim):
    pieces = jnp.moveaxis(pieces, 0, dim)
    shape = pieces.shape
    return pieces.reshape(*shape[:dim], shape[dim] * shape[dim + 1], *shape[dim + 2 :])


def all_blocks(shard, axes, sequence):
    pieces = shard[None]
    for k in sequence:
        pieces = lax.all_gather(pieces, axes[k], axis=0, tiled=True)
    held = [lax.axis_size(axes[k]) for k in reversed(sequence)]
    pieces = pieces.reshape(*held, *shard.shape)
    turned = sorted(range(len(sequence)), key=lambda place: sequence[len(sequence) - 1 - place])
    return pieces.transpose(*turned, *range(len(sequence), pieces.ndim)).reshape(-1, *shard.shape)


def gathered_by_axis(shard, axes, sequence, dim):
    return laid_out(all_blocks(shard, axes, sequence), dim)


def swapped(shard, axis, stride):
    return lax.ppermute(shard, axis, [(i, i ^ 1 << stride) for i in range(lax.axis_size(axis))])


def split_up(shard, dim, count):
    shape = shard.shape
    pieces = shard.reshape(*shape[:dim], count, shape[dim] // count, *shape[dim + 1 :])
    return jnp.moveaxis(pieces, dim, 0)


def sent_and_summed(shard, axis, dim):
    count = lax.axis_size(axis)
    pieces = lax.all_to_all(split_up(shard, dim, count), axis, 0, 0, tiled=True)
    return jnp.sum(pieces, axis=0)


def summed_rows(shard, axes, dim):
    far, near = axes
    return sent_and_summed(sent_and_summed(shard, far, dim), near, dim)


def from_behind(block, axis, distance):
    devices = range(lax.axis_size(axis))
    route = [(i - distance, i) for i in devices if i - distance in devices]
    return lax.ppermute(block, axis, route)


def sent_to_all(shard, axis):
    count = lax.axis_size(axis)
    return lax.all_to_all(
        jnp.broadcast_to(shard[None], (count, *shard.shape)), axis, 0, 0, tiled=True
    )


def gathered_copies(shard, axis, dim):
    return laid_out(sent_to_all(shard, axis), dim)


def in_one_piece(arrays, axis, dim, along):
    ends, at = ([], 0)
    for a in arrays[:-1]:
        at += a.shape[along]
        ends.append(at)
    both = jnp.concatenate(arrays, axis=along)
    return tuple(jnp.split(gathered_copies(both, axis, dim), ends, axis=along))


def contract_rows(left_rows, right_rows):
    return lax.dot_general(
        left_rows, right_rows, (((0,), (0,)), ((), ())), preferred_element_type=jnp.float32
    )


def contract_cols(left_rows, right_rows):
    return lax.dot_general(
        left_rows, right_rows, (((1,), (1,)), ((), ())), preferred_element_type=jnp.float32
    )


def on_device(resid, target, enc_weight, enc_bias, dec_weight, blocks):
    latent_devices = lax.axis_size(LATENT)
    layer_slot = lax.axis_index("layer")
    layer_row = layer_slot // 2
    which_half = layer_slot % 2
    column_pos = lax.axis_index(LATENT)
    rows_in = lax.dynamic_index_in_dim(resid, layer_row, 0, keepdims=False)
    local_rows = rows_in.shape[0]
    token_count = local_rows * latent_devices
    weight_in = enc_weight[0]
    block_width = weight_in.shape[1]
    decoder = dec_weight[0]
    column_width = decoder.shape[-1]
    dec_own = decoder[0].reshape(2 * block_width, column_width)
    dec_next = decoder[1].reshape(2 * block_width, column_width)
    listed = lax.dynamic_index_in_dim(blocks, layer_row, 0, keepdims=False)
    tile_len = token_count // listed.shape[0]
    flags = jnp.any(listed == which_half * latent_devices + column_pos, axis=1).astype(jnp.float32)
    gate_mask = jnp.repeat(flags, tile_len)[:, None]
    whole_in = gathered_by_axis(rows_in, LATENT, (0, 1), 0)
    preact = jnp.dot(whole_in, weight_in, preferred_element_type=jnp.float32)
    preact = preact + enc_bias[0][None, :]
    latents_on = (preact * gate_mask).astype(jnp.bfloat16)
    partner = swapped(latents_on, "layer", 0)
    lower_half = jnp.where(which_half == 0, latents_on, partner)
    upper_half = jnp.where(which_half == 0, partner, latents_on)
    pair_acts = jnp.concatenate([lower_half, upper_half], axis=1)
    totals = summed_rows(
        jnp.concatenate(
            [
                jnp.dot(pair_acts, dec_own, preferred_element_type=jnp.float32),
                jnp.dot(pair_acts, dec_next, preferred_element_type=jnp.float32),
            ],
            axis=1,
        ),
        ("latent_0", "latent_1"),
        0,
    )
    own_sum = totals[:, :column_width]
    ahead_part = totals[:, column_width:]
    targets = lax.dynamic_slice_in_dim(target, layer_row, 2, 0)
    targets = lax.dynamic_slice_in_dim(targets, which_half * column_width, column_width, 2).astype(
        jnp.float32
    )
    behind = from_behind(ahead_part, "layer", 2)
    err_own = (own_sum + behind - targets[0]).astype(jnp.bfloat16)
    next_own = from_behind(own_sum, "layer", -2)
    err_next = (next_own + ahead_part - targets[1]).astype(jnp.bfloat16)
    piece_pair = in_one_piece((err_own, err_next), LATENT, 0, 1)
    grad_pair = contract_cols(piece_pair[0], dec_own) + contract_cols(piece_pair[1], dec_next)
    lower_grad = grad_pair[:, :block_width]
    upper_grad = grad_pair[:, block_width:]
    own_part = jnp.where(which_half == 0, lower_grad, upper_grad)
    their_part = jnp.where(which_half == 0, upper_grad, lower_grad)
    received = swapped(their_part, "layer", 0)
    grad_pre = (own_part + received) * gate_mask
    bias_grad = jnp.sum(grad_pre, axis=0)[None, :]
    grad_low = grad_pre.astype(jnp.bfloat16)
    grad_weight = contract_rows(whole_in, grad_low)
    return (err_own[None], grad_weight.astype(jnp.bfloat16)[None], bias_grad)


def solution(mesh):
    finer = Mesh(
        mesh.devices.reshape(mesh.shape["layer"], 4, 16), ("layer", "latent_0", "latent_1")
    )
    placed = (
        P(None, LATENT, None),
        P(None, LATENT, None),
        P("layer", None, LATENT),
        P("layer", LATENT),
        P("layer", None, None, LATENT, None),
        P(),
    )
    return jax.shard_map(
        on_device,
        mesh=finer,
        in_specs=placed,
        out_specs=(P("layer", LATENT, None), P("layer", None, LATENT), P("layer", LATENT)),
        check_vma=False,
    )
```

profile of v0, /device:TPU:1, one launch (start us, length us, event | category | flops | bytes accessed | tf_op | source)
XLA Modules:
  0.0 202.1 jit_solution(11026004268313117025)
XLA Ops:
  0.6 0.0 copy-start
  0.7 0.8 constant_dynamic-slice_fusion.1
  1.5 10.2 %all_gather.6 = bf16[4,2,3584]{2,1,0:T(2,128)(2,1)S(1)} all-gather(bf16[1,2,3584]{2,1,0:T(2,128)(2,1)S(1)} %constant_dynamic-slice_fusion.1), channel_id=1, replica_groups=mesh['layer'=8,'latent_0'=4,'latent_1'=16] {'latent_0'}, dimensions={0}, use_global_device_ids=true | all-gather | bytes 71680 | tf_op jit(solution)/shard_map/all_gather | solution.py:19
  11.6 34.1 %all_gather.7 = bf16[64,2,3584]{2,1,0:T(2,128)(2,1)S(1)} all-gather(bf16[4,2,3584]{2,1,0:T(2,128)(2,1)S(1)} %all_gather.6), channel_id=1, replica_groups=mesh['layer'=8,'latent_0'=4,'latent_1'=16] {'latent_1'}, dimensions={0}, use_global_device_ids=true | all-gather | bytes 974848 | tf_op jit(solution)/shard_map/all_gather | solution.py:19
  45.7 0.6 copy.30
  46.4 0.3 reshape_reshape.3
  46.7 1.3 compare_reduce_fusion
  48.7 0.5 fusion.2
  49.2 12.2 %collective-permute-start = (bf16[128,128]{0,1:T(8,128)(2,1)S(1)}, bf16[128,128]{0,1:T(8,128)(2,1)S(1)}, u32[]{:S(2)}, u32[]{:S(2)}) collective-permute-start(bf16[128,128]{0,1:T(8,128)(2,1)S(1)} %fusion.2), channel_id=1, source_target_pairs={{0,64},{64,0},{128,192},{192,128},{256,320},{320,256},{384,448},{4... | collective-permute-start | bytes 98312 | tf_op jit(solution)/shard_map/ppermute | solution.py:31
  61.4 1.0 fusion.17
  62.4 1.5 fusion.8
  63.9 0.3 fusion.7
  64.2 0.2 pad_maximum_fusion
  64.4 26.5 %all_to_all.15 = f32[4,32,3584]{2,1,0:T(8,128)} all-to-all(f32[4,32,3584]{2,1,0:T(8,128)S(1)} %bitcast.38), channel_id=1, replica_groups=mesh['layer'=8,'latent_0'=4,'latent_1'=16] {'latent_0'}, dimensions={0} | all-to-all | bytes 3670016 | tf_op jit(solution)/shard_map/all_to_all | solution.py:42
  91.0 1.6 reduce_sum.27
  92.6 1.0 reshape.43
  93.6 6.7 %all-to-all-start.1 = ((f32[16,2,3584]{2,1,0:T(2,128)}), f32[16,2,3584]{2,1,0:T(2,128)S(1)}, u32[]{:S(2)}, u32[]{:S(2)}) async-start(f32[16,2,3584]{2,1,0:T(2,128)} %reshape.43), calls=%async_computation.1 | async-start | bytes 917504 | tf_op jit(solution)/shard_map/all_to_all | solution.py:42
  100.4 20.8 %all-to-all-done.1 = f32[16,2,3584]{2,1,0:T(2,128)S(1)} async-done(((f32[16,2,3584]{2,1,0:T(2,128)}), f32[16,2,3584]{2,1,0:T(2,128)S(1)}, u32[]{:S(2)}, u32[]{:S(2)}) %all-to-all-start.1) | async-done | bytes 458784 | tf_op jit(solution)/shard_map/all_to_all | solution.py:42
  121.3 0.1 reduce_sum.28
  121.4 3.2 %collective-permute-start.1 = (f32[2,1792]{1,0:T(2,128)S(1)}, f32[2,1792]{1,0:T(2,128)S(1)}, u32[]{:S(2)}, u32[]{:S(2)}) collective-permute-start(f32[2,1792]{1,0:T(2,128)S(1)} %get-tuple-element.12), channel_id=1, source_target_pairs={{0,128},{64,192},{128,256},{192,320},{256,384},{320,448},{1,129},{... | collective-permute-start | bytes 43016 | tf_op jit(solution)/shard_map/ppermute | solution.py:54
  124.6 1.3 collective-permute-start.2
  125.9 0.8 dynamic-slice_convert_fusion
  126.7 2.3 %collective-permute-done.2 = f32[2,1792]{1,0:T(2,128)S(1)} collective-permute-done((f32[2,1792]{1,0:T(2,128)S(1)}, f32[2,1792]{1,0:T(2,128)S(1)}, u32[]{:S(2)}, u32[]{:S(2)}) %collective-permute-start.2) | collective-permute-done | bytes 14368 | tf_op jit(solution)/shard_map/ppermute | solution.py:54
  129.1 0.5 broadcast_in_dim.18
  129.6 56.9 %all_to_all.16 = bf16[64,2,3584]{2,1,0:T(2,128)(2,1)} all-to-all(bf16[64,2,3584]{2,1,0:T(2,128)(2,1)S(1)} %broadcast_in_dim.18), channel_id=1, replica_groups=mesh['layer'=8,'latent_0'=4,'latent_1'=16] {'latent_0','latent_1'}, dimensions={0} | all-to-all | bytes 1835008 | tf_op jit(solution)/shard_map/all_to_all | solution.py:59
  186.5 3.2 %reshape.44 = bf16[128,3584]{1,0:T(8,128)(2,1)} reshape(bf16[64,2,3584]{2,1,0:T(2,128)(2,1)} %all_to_all.16) | data formatting | bytes 1835008 | tf_op jit(solution)/shard_map/reshape | solution.py:13
  189.7 1.7 fusion.5
  191.4 1.4 convolution_add_fusion
  192.8 6.4 %collective-permute-start.3 = (f32[128,128]{0,1:T(8,128)S(1)}, f32[128,128]{0,1:T(8,128)S(1)}, u32[]{:S(2)}, u32[]{:S(2)}) collective-permute-start(f32[128,128]{0,1:T(8,128)S(1)} %slice_select_fusion), channel_id=1, source_target_pairs={{0,64},{64,0},{128,192},{192,128},{256,320},{320,256},{384,448},{4... | collective-permute-start | bytes 196616 | tf_op jit(solution)/shard_map/ppermute | solution.py:31
  199.3 0.9 collective-permute-done.3
  200.2 0.6 fusion.16
  200.8 1.4 fusion
  (14 shorter events, 0.1 us)
Async XLA Ops:
  0.6 48.1 %copy-start = (bf16[1,3584,128]{2,1,0:T(8,128)(2,1)S(1)}, bf16[1,3584,128]{2,1,0:T(8,128)(2,1)}, u32[]{:S(2)}) copy-start(bf16[1,3584,128]{2,1,0:T(8,128)(2,1)} %param.8) | copy-start | bytes 2752516
  45.7 3.0 %copy-start.3 = (f32[1,128]{1,0:T(1,128)S(1)}, f32[1,128]{1,0:T(1,128)}, u32[]{:S(2)}) copy-start(f32[1,128]{1,0:T(1,128)} %param.9) | copy-start | bytes 1540
  48.7 12.7 %copy-start.1 = (bf16[1,2,2,128,1792]{4,3,2,1,0:T(8,128)(2,1)S(1)}, bf16[1,2,2,128,1792]{4,3,2,1,0:T(8,128)(2,1)}, u32[]{:S(2)}) copy-start(bf16[1,2,2,128,1792]{4,3,2,1,0:T(8,128)(2,1)} %param.10) | copy-start | bytes 5505028
  49.2 13.2 %collective-permute-start = (bf16[128,128]{0,1:T(8,128)(2,1)S(1)}, bf16[128,128]{0,1:T(8,128)(2,1)S(1)}, u32[]{:S(2)}, u32[]{:S(2)}) collective-permute-start(bf16[128,128]{0,1:T(8,128)(2,1)S(1)} %fusion.2), channel_id=1, source_target_pairs={{0,64},{64,0},{128,192},{192,128},{256,320},{320,256},{384,448},{4... | collective-permute-start | bytes 98312 | tf_op jit(solution)/shard_map/ppermute | solution.py:31
  93.6 27.6 %all-to-all-start.1 = ((f32[16,2,3584]{2,1,0:T(2,128)}), f32[16,2,3584]{2,1,0:T(2,128)S(1)}, u32[]{:S(2)}, u32[]{:S(2)}) async-start(f32[16,2,3584]{2,1,0:T(2,128)} %reshape.43), calls=%async_computation.1 | async-start | bytes 917504 | tf_op jit(solution)/shard_map/all_to_all | solution.py:42
  121.4 5.3 %collective-permute-start.1 = (f32[2,1792]{1,0:T(2,128)S(1)}, f32[2,1792]{1,0:T(2,128)S(1)}, u32[]{:S(2)}, u32[]{:S(2)}) collective-permute-start(f32[2,1792]{1,0:T(2,128)S(1)} %get-tuple-element.12), channel_id=1, source_target_pairs={{0,128},{64,192},{128,256},{192,320},{256,384},{320,448},{1,129},{... | collective-permute-start | bytes 43016 | tf_op jit(solution)/shard_map/ppermute | solution.py:54
  124.6 4.5 %collective-permute-start.2 = (f32[2,1792]{1,0:T(2,128)S(1)}, f32[2,1792]{1,0:T(2,128)S(1)}, u32[]{:S(2)}, u32[]{:S(2)}) collective-permute-start(f32[2,1792]{1,0:T(2,128)S(1)} %get-tuple-element.11), channel_id=1, source_target_pairs={{128,0},{192,64},{256,128},{320,192},{384,256},{448,320},{129,1},{... | collective-permute-start | bytes 43016 | tf_op jit(solution)/shard_map/ppermute | solution.py:54
  129.1 60.6 %copy-start.2 = (bf16[2,1792]{1,0:T(2,128)(2,1)}, bf16[2,1792]{1,0:T(2,128)(2,1)S(1)}, u32[]{:S(2)}) copy-start(bf16[2,1792]{1,0:T(2,128)(2,1)S(1)} %get-tuple-element.10) | copy-start | bytes 21508
  192.8 7.3 %collective-permute-start.3 = (f32[128,128]{0,1:T(8,128)S(1)}, f32[128,128]{0,1:T(8,128)S(1)}, u32[]{:S(2)}, u32[]{:S(2)}) collective-permute-start(f32[128,128]{0,1:T(8,128)S(1)} %slice_select_fusion), channel_id=1, source_target_pairs={{0,64},{64,0},{128,192},{192,128},{256,320},{320,256},{384,448},{4... | collective-permute-start | bytes 196616 | tf_op jit(solution)/shard_map/ppermute | solution.py:31
where the time goes:
time: 203 us; the launch traced here: 202 us
  blocking collectives  128 us (63%)
  starting transfers between devices  29.8 us (15%)
  waiting for transfers between devices  24.1 us (12%)
  local copies, waits for them, and re-layouts  7.57 us (4%)
  matrix products  6.75 us (3%)
  other arithmetic  4.76 us (2%)
    all_to_all x1, blocking collectives, sent_to_all(): lax.all_to_all(jnp.broadcast_to(shard[None], (count, *shard.shape)), axis...  56.9 us
    all_gather x2, blocking collectives, all_blocks(): pieces = lax.all_gather(pieces, axes[k], axis=0, tiled=True)  44.3 us
    all_to_all x1, blocking collectives, sent_and_summed(): pieces = lax.all_to_all(split_up(shard, dim, count), axis, 0, 0, tiled=True)  26.5 us
    all_to_all x1, waiting for transfers between devices, sent_and_summed(): pieces = lax.all_to_all(split_up(shard, dim, count), axis, 0, 0, tiled=True)  20.8 us
    ppermute x2, starting transfers between devices, swapped(): lax.ppermute(shard, axis, [(i, i ^ 1 << stride) for i in range(lax.axis_s...  18.6 us
    all_to_all x1, starting transfers between devices, sent_and_summed(): pieces = lax.all_to_all(split_up(shard, dim, count), axis, 0, 0, tiled=True)  6.74 us
    ppermute x2, starting transfers between devices, from_behind(): return lax.ppermute(block, axis, route)  4.47 us
  transfers between devices with their start and end apart: 5, of which 3 were waited for; matrix products, arithmetic and copies ran while one was open for 1% of the time, Pallas kernels for 0%

commit v1 on v0

v1 whole, which is shorter than its diff:
```python
import functools

import jax
import jax.numpy as jnp
from jax import lax
from jax.experimental import pallas as pl
from jax.experimental.pallas import tpu as pltpu
from jax.sharding import Mesh
from jax.sharding import PartitionSpec as P

NY, NX, NZ = 4, 4, 16
NA = 4
F32, BF16 = jnp.float32, jnp.bfloat16
SENDS = 160
FAR_GREETING = True


def body(
    resid, target, enc, bias, dec, blocks,
    x_out, low_out, bias_out, err_out,
    X, XO, XS, WE, BI, DW, TG, PP, PR, S0, S1, R0, R1, B0, B1, Q0, Q1,
    S2, S2F, R2, YO, YA, YN, YB, E, EM, GP, GR, loc, ssem, rsem,
):
    y, h = lax.axis_index("y"), lax.axis_index("core")
    x, z = lax.axis_index("x"), lax.axis_index("z")
    other = 1 - h
    r, a = lax.rem(z, 4), lax.div(z, 4)
    half = XO.shape[-1]
    width = bias.shape[-1]

    def at_x(d):
        return {"x": lax.rem(x + d, NX)}

    def at_z(d):
        return {"z": lax.rem(z + d + NZ, NZ)}

    sibling = {"core": other}

    barrier = pltpu.get_barrier_semaphore()
    near = [sibling, at_x(1), at_x(2), at_x(3), at_z(1), at_z(-1)]
    if FAR_GREETING:
        near += [at_z(d) for d in (2, -2, 4, -4, 8)]
    for peer in near:
        pl.semaphore_signal(barrier, inc=1, device_id=peer, device_id_type=pl.DeviceIdType.MESH)

    @pl.when(y > 0)
    def _():
        pl.semaphore_signal(barrier, inc=1, device_id={"y": y - 1}, device_id_type=pl.DeviceIdType.MESH)

    @pl.when(y < NY - 1)
    def _():
        pl.semaphore_signal(barrier, inc=1, device_id={"y": y + 1}, device_id_type=pl.DeviceIdType.MESH)

    mine = resid.at[y, :, pl.ds(pl.multiple_of(h * half, 128), half)]
    keep = pltpu.make_async_copy(mine, X.at[r, x, a], loc.at[0])
    keep.start()
    enc_own = pltpu.make_async_copy(
        enc.at[0, pl.ds(pl.multiple_of(h * half, 128), half), :],
        WE.at[:, pl.ds(pl.multiple_of(h * width, 128), width)], loc.at[1])
    enc_own.start()
    bias_own = pltpu.make_async_copy(bias, BI.at[h], loc.at[2])
    bias_own.start()
    tgt = pltpu.make_async_copy(
        target.at[pl.ds(y, 2), :, pl.ds(pl.multiple_of(h * half, 128), half)], TG, loc.at[3])
    tgt.start()
    dec_in = pltpu.make_async_copy(dec.at[0], DW, loc.at[4])
    dec_in.start()

    extra = jnp.where(jnp.logical_and(y > 0, y < NY - 1), 2, 1)
    pl.semaphore_wait(barrier, len(near) + extra)

    count = [0]
    started = []

    def made(src, dst, peer):
        k = count[0]
        count[0] += 1
        return pltpu.make_async_remote_copy(
            src_ref=src, dst_ref=dst, send_sem=ssem.at[k], recv_sem=rsem.at[k],
            device_id=peer, device_id_type=pl.DeviceIdType.MESH)

    def send(src, dst, peer):
        copy = made(src, dst, peer)
        copy.start()
        started.append(copy)
        return copy

    def slot(d):
        zz = lax.rem(z + d + NZ, NZ)
        return lax.rem(zz, 4), lax.div(zz, 4)

    up = send(mine, X.at[r, x, a], at_z(1))
    down = send(mine, X.at[r, x, a], at_z(-1))
    across = [send(mine, X.at[r, x, a], at_x(d)) for d in (2, 1, 3)]
    enc_far = send(
        enc.at[0, pl.ds(pl.multiple_of(other * half, 128), half), :],
        WE.at[:, pl.ds(pl.multiple_of(h * width, 128), width)], sibling)
    bias_far = send(bias, BI.at[h], sibling)
    for s in range(1, 9):
        up.wait_recv()
        rr, aa = slot(-s)
        got = X.at[rr, x, aa]
        if s < 8:
            up = send(got, got, at_z(1))
        across += [send(got, got, at_x(d)) for d in (2, 1, 3)]
        if s < 8:
            down.wait_recv()
            rr, aa = slot(s)
            got = X.at[rr, x, aa]
            if s < 7:
                down = send(got, got, at_z(-1))
            across += [send(got, got, at_x(d)) for d in (2, 1, 3)]

    row = blocks[y]
    column = x * NZ + z
    hits = [
        jnp.max((row == g * NX * NZ + column).astype(F32), axis=1, keepdims=True)
        for g in range(2)
    ]
    lanes = lax.broadcasted_iota(jnp.int32, (1, 2 * width), 1)
    gates = jnp.where(lanes < width, hits[0], hits[1])
    gate_own = jnp.where(h == 0, hits[0], hits[1])

    bias_far.wait_recv()
    bias_own.wait()
    enc_far.wait_recv()
    enc_own.wait()
    keep.wait()
    for copy in across:
        copy.wait_recv()
    rows = 4 * NX * NA * 2
    for rr in range(4):
        XO[pl.ds(rr * 32, 32), :] = X[rr].reshape(32, half)
    PP[...] = jnp.dot(XO[...], WE[...], preferred_element_type=F32)
    part = send(PP, PR, sibling)
    rows_far = send(XO, XS, sibling)
    part.wait_recv()
    biases = jnp.concatenate([BI[0], BI[1]], axis=1)
    acts = ((PP[...] + PR[...] + biases) * gates).astype(BF16)

    dec_in.wait()
    step = 256
    for t, S in ((1, S1), (0, S0)):
        for n in range(0, half, step):
            w = DW[t, :, :, n:n + step].reshape(2 * width, step)
            p = jnp.dot(acts, w, preferred_element_type=F32)
            S[:, :, :, n:n + step] = p.reshape(4, NX, 8, step).astype(BF16)
        if t == 1:
            r1, r3, r2 = lax.rem(r + 1, 4), lax.rem(r + 3, 4), lax.rem(r + 2, 4)
            in1 = [
                send(S1.at[r2, pl.ds(0, 2)], R1.at[2, pl.ds(0, 2)], at_z(2)),
                send(S1.at[r2, pl.ds(2, 2)], R1.at[2, pl.ds(2, 2)], at_z(-2)),
                send(S1.at[r1], R1.at[0], at_z(1)),
                send(S1.at[r3], R1.at[1], at_z(-1)),
            ]
        else:
            in0 = [
                send(S0.at[:, lax.rem(x + d, NX)], R0.at[i], at_x(d))
                for i, d in enumerate((2, 1, 3))
            ]
    for copy in in1:
        copy.wait_recv()

    def summed1(xx):
        return (S1[r, xx].astype(F32) + R1[0, xx].astype(F32)) + (
            R1[1, xx].astype(F32) + R1[2, xx].astype(F32))

    def summed0(rr):
        return (S0[rr, x].astype(F32) + R0[0, rr].astype(F32)) + (
            R0[1, rr].astype(F32) + R0[2, rr].astype(F32))

    next1 = []
    for i, d in enumerate((2, 1, 3)):
        B1[i] = summed1(lax.rem(x + d, NX)).astype(BF16)
        next1.append(send(B1.at[i], Q1.at[i], at_x(d)))
    for copy in in0:
        copy.wait_recv()
    next0 = []
    n2 = half // 2
    B0[2] = summed0(r2).astype(BF16)
    next0.append(send(B0.at[2, :, pl.ds(0, n2)], Q0.at[2, :, pl.ds(0, n2)], at_z(2)))
    next0.append(send(B0.at[2, :, pl.ds(n2, n2)], Q0.at[2, :, pl.ds(n2, n2)], at_z(-2)))
    B0[0] = summed0(r1).astype(BF16)
    next0.append(send(B0.at[0], Q0.at[0], at_z(1)))
    B0[1] = summed0(r3).astype(BF16)
    next0.append(send(B0.at[1], Q0.at[1], at_z(-1)))
    own1 = summed1(x)
    own0 = summed0(r)
    for copy in next1 + next0:
        copy.wait_recv()
    for t, own, Q in ((0, own0, Q0), (1, own1, Q1)):
        total = (own + Q[0].astype(F32)) + (Q[1].astype(F32) + Q[2].astype(F32))
        for aa in range(NA):
            two = total[2 * aa:2 * aa + 2, :]
            S2F[aa, t] = two
            S2[aa, t] = two.astype(BF16)
    last = [
        send(S2.at[lax.rem(a + d, NA)], R2.at[i], at_z(4 * d if d < 3 else -4))
        for i, d in enumerate((2, 1, 3))
    ]
    for copy in last:
        copy.wait_recv()
    sums = S2F[a] + R2[0].astype(F32) + R2[1].astype(F32) + R2[2].astype(F32)
    YO[...] = sums[0]
    YA[...] = sums[1]

    up_y = made(YA, YB, {"y": lax.rem(y + 1, NY)})
    down_y = made(YO, YN, {"y": lax.rem(y + NY - 1, NY)})

    @pl.when(y < NY - 1)
    def _():
        up_y.start()

    @pl.when(y > 0)
    def _():
        down_y.start()
        up_y.wait_recv()

    @pl.when(y == 0)
    def _():
        YB[...] = jnp.zeros_like(YB)

    @pl.when(y < NY - 1)
    def _():
        down_y.wait_recv()

    @pl.when(y == NY - 1)
    def _():
        YN[...] = jnp.zeros_like(YN)

    tgt.wait()
    err_own = (sums[0] + YB[...] - TG[0].astype(F32)).astype(BF16)
    err_next = (YN[...] + sums[1] - TG[1].astype(F32)).astype(BF16)
    err_out[0] = err_own
    E[0, r, x, a] = err_own
    E[1, r, x, a] = err_next

    piece = E.at[:, r, x, a]
    gathered = [send(piece, piece, at_z(d)) for d in (8, 4, -4)]
    for copy in gathered:
        copy.wait_recv()
    h2 = NA // 2

    def along_x(t, rr):
        block = E.at[t, rr, x]
        return [send(block, block, at_x(d)) for d in (2, 1, 3)]

    def along_z(t, xx):
        lo, hi = E.at[t, r, xx, pl.ds(0, h2)], E.at[t, r, xx, pl.ds(h2, h2)]
        block = E.at[t, r, xx]
        return [
            send(lo, lo, at_z(-2)), send(hi, hi, at_z(2)),
            send(block, block, at_z(-1)), send(block, block, at_z(1)),
        ]

    first0 = along_z(0, x)
    first1 = along_x(1, r)
    rest = along_x(0, r) + along_z(1, x)
    for d, copy in zip((2, 1, 3), first1):
        copy.wait_recv()
        rest += along_z(1, lax.rem(x + NX - d, NX))
    first0[2].wait_recv()
    rest += along_x(0, r1)
    first0[3].wait_recv()
    rest += along_x(0, r3)
    first0[0].wait_recv()
    first0[1].wait_recv()
    rest += along_x(0, r2)
    for copy in rest:
        copy.wait_recv()
    grad = None
    for t in range(2):
        for rr in range(4):
            EM[pl.ds(rr * 32, 32), :] = E[t, rr].reshape(32, half)
        term = lax.dot_general(
            EM[...], DW[t].reshape(2 * width, half), (((1,), (1,)), ((), ())),
            preferred_element_type=F32)
        grad = term if grad is None else grad + term
    GP[0] = grad[:, :width]
    GP[1] = grad[:, width:]
    back = send(GP.at[other], GR, sibling)

    rows_far.wait_recv()
    out_a = pltpu.make_async_copy(XO, x_out.at[h], loc.at[5])
    out_b = pltpu.make_async_copy(XS, x_out.at[other], loc.at[6])
    out_a.start()
    out_b.start()
    back.wait_recv()
    grad_pre = (GP[h] + GR[...]) * gate_own
    bias_out[...] = jnp.sum(grad_pre, axis=0, keepdims=True)
    low_out[...] = grad_pre.astype(BF16)
    for copy in started:
        copy.wait_send()

    @pl.when(y < NY - 1)
    def _():
        up_y.wait_send()

    @pl.when(y > 0)
    def _():
        down_y.wait_send()

    out_a.wait()
    out_b.wait()


def on_device(resid, target, enc, bias, dec, blocks):
    half = dec.shape[-1]
    width = enc.shape[-1]
    rows = 128
    any_spec = pl.BlockSpec(memory_space=pl.ANY)
    vmem = pl.BlockSpec(memory_space=pltpu.VMEM)
    V = pltpu.VMEM
    x_all, low, bias_grad, errors = pl.pallas_call(
        body,
        out_shape=(
            jax.ShapeDtypeStruct((2, rows, half), BF16),
            jax.ShapeDtypeStruct((rows, width), BF16),
            jax.ShapeDtypeStruct((1, width), F32),
            jax.ShapeDtypeStruct((1, 2, half), BF16),
        ),
        in_specs=[any_spec] * 5 + [vmem],
        out_specs=(any_spec, vmem, vmem, vmem),
        scratch_shapes=[
            V((4, NX, NA, 2, half), BF16),
            V((rows, half), BF16),
            V((rows, half), BF16),
            V((half, 2 * width), BF16),
            V((2, 1, width), F32),
            V((2, 2, width, half), BF16),
            V((2, 2, half), BF16),
            V((rows, 2 * width), F32),
            V((rows, 2 * width), F32),
            V((4, NX, 8, half), BF16),
            V((4, NX, 8, half), BF16),
            V((3, 4, 8, half), BF16),
            V((3, NX, 8, half), BF16),
            V((3, 8, half), BF16),
            V((3, 8, half), BF16),
            V((3, 8, half), BF16),
            V((3, 8, half), BF16),
            V((NA, 2, 2, half), BF16),
            V((NA, 2, 2, half), F32),
            V((3, 2, 2, half), BF16),
            V((2, half), F32),
            V((2, half), F32),
            V((2, half), F32),
            V((2, half), F32),
            V((2, 4, NX, NA, 2, half), BF16),
            V((rows, half), BF16),
            V((2, rows, width), F32),
            V((rows, width), F32),
            pltpu.SemaphoreType.DMA((8,)),
            pltpu.SemaphoreType.DMA((SENDS,)),
            pltpu.SemaphoreType.DMA((SENDS,)),
        ],
        compiler_params=pltpu.CompilerParams(collective_id=0, has_side_effects=True),
        name="step",
    )(resid, target, enc, bias, dec, blocks)
    grad = lax.dot_general(
        x_all, low, (((1,), (0,)), ((), ())), preferred_element_type=F32)
    return errors, grad.astype(BF16).reshape(1, 2 * half, width), bias_grad


def solution(mesh):
    fine = Mesh(mesh.devices.reshape(NY, 2, NX, NZ), ("y", "core", "x", "z"))
    layer, latent = ("y", "core"), ("x", "z")
    return jax.shard_map(
        on_device,
        mesh=fine,
        in_specs=(
            P(None, latent, None), P(None, latent, None), P(layer, None, latent),
            P(layer, latent), P(layer, None, None, latent, None), P(),
        ),
        out_specs=(P(layer, latent, None), P(layer, None, latent), P(layer, latent)),
        check_vma=False,
    )
```

time: 203 us -> 92.4 us (0.46)
  blocking collectives: 128 us -> 0 us
  Pallas kernels: 0 us -> 88 us
  starting transfers between devices: 29.8 us -> 0 us
  waiting for transfers between devices: 24.1 us -> 0 us
  local copies, waits for them, and re-layouts: 7.57 us -> 1.11 us
  other arithmetic: 4.76 us -> 0 us
  matrix products: 6.75 us -> 2.54 us
    pallas_call x0 -> x1, Pallas kernels: none -> 88 us  [on_device(): pl.pallas_call(body, out_shape=(jax.ShapeDtypeStruct((2, rows, half), BF1...]
    all_to_all x2 -> x0, blocking collectives: 83.4 us -> none  [the longest x1 56.9 us: sent_to_all(): lax.all_to_all(jnp.broadcast_to(shard[None], (count, *shard.shape)), axis...]
    all_gather x2 -> x0, blocking collectives: 44.3 us -> none  [all_blocks(): pieces = lax.all_gather(pieces, axes[k], axis=0, tiled=True)]
    ppermute x4 -> x0, starting transfers between devices: 23.1 us -> none  [the longest x2 18.6 us: swapped(): lax.ppermute(shard, axis, [(i, i ^ 1 << stride) for i in range(lax.axis_s...]
    all_to_all x1 -> x0, waiting for transfers between devices: 20.8 us -> none  [sent_and_summed(): pieces = lax.all_to_all(split_up(shard, dim, count), axis, 0, 0, tiled=True)]
    all_to_all x1 -> x0, starting transfers between devices: 6.74 us -> none  [sent_and_summed(): pieces = lax.all_to_all(split_up(shard, dim, count), axis, 0, 0, tiled=True)]
    reshape x3 -> x0, local copies, waits for them, and re-layouts: 4.86 us -> none  [the longest x1 3.19 us: laid_out(): pieces.reshape(*shape[:dim], shape[dim] * shape[dim + 1], *shape[dim + 2:])]
    dot_general x6 -> x1, matrix products: 6.75 us -> 2.54 us  [on_device(): lax.dot_general(x_all, low, (((1,), (0,)), ((), ())), preferred_element_t...]
  transfers between devices with their start and end apart: 5 -> 0, of which waited for: 3 -> 0; matrix products, arithmetic and copies ran while one was open for 1% -> 0% of each run, Pallas kernels for 0% -> 0%
where the time goes in v1:
time: 92.4 us; the launch traced here: 92.3 us
  Pallas kernels  88 us (95%)
  matrix products  2.54 us (3%)
  local copies, waits for them, and re-layouts  1.11 us (1%)
    pallas_call x1, Pallas kernels, on_device(): pl.pallas_call(body, out_shape=(jax.ShapeDtypeStruct((2, rows, half), BF1...  88 us
    dot_general x1, matrix products, on_device(): lax.dot_general(x_all, low, (((1,), (0,)), ((), ())), preferred_element_t...  2.54 us

profile of v1, /device:TPU:1, one launch (start us, length us, event | category | flops | bytes accessed | tf_op | source)
XLA Modules:
  0.0 92.3 jit_solution(2058350065698376946)
XLA Ops:
  0.6 88.0 %step.1 = (bf16[2,128,1792]{2,1,0:T(8,128)(2,1)}, bf16[128,128]{1,0:T(8,128)(2,1)}, f32[1,128]{1,0:T(1,128)}, bf16[1,2,1792]{2,1,0:T(2,128)(2,1)}) custom-call(bf16[4,2,3584]{2,1,0:T(2,128)(2,1)} %resid.1, bf16[5,2,3584]{2,1,0:T(2,128)(2,1)} %target.1, bf16[1,3584,128]{2,1,0:T(8,128)(2,1)} %enc.1, f32[1,128]{1,0:T(1,128)} %bias.1, ...), custom_call_target="tpu_custom_call" | custom-call | tf_op jit(solution)/shard_map/step/pallas_call | solution.py:314
  88.6 0.0 copy-start
  88.6 0.0 copy-start.1
  88.6 2.5 %convolution_convert_fusion = bf16[2,1792,128]{2,1,0:T(8,128)(2,1)} fusion(bf16[2,128,1792]{2,1,0:T(8,128)(2,1)} %get-tuple-element.8, bf16[128,128]{1,0:T(8,128)(2,1)} %get-tuple-element.9), kind=kOutput, calls=%fused_computation | convolution fusion | flops 117899264 | bytes 1867776 | tf_op jit(solution)/shard_map/dot_general | solution.py:360
  91.2 0.0 copy-done
  91.2 0.6 copy.13
  91.8 0.0 copy-done.1
  91.8 0.5 copy.14
Async XLA Ops:
  88.6 2.6 %copy-start = (bf16[1,2,1792]{2,1,0:T(2,128)(2,1)S(1)}, bf16[1,2,1792]{2,1,0:T(2,128)(2,1)}, u32[]{:S(2)}) copy-start(bf16[1,2,1792]{2,1,0:T(2,128)(2,1)} %get-tuple-element.14) | copy-start | bytes 21508
  88.6 3.2 %copy-start.1 = (f32[1,128]{1,0:T(1,128)S(1)}, f32[1,128]{1,0:T(1,128)}, u32[]{:S(2)}) copy-start(f32[1,128]{1,0:T(1,128)} %get-tuple-element.16) | copy-start | bytes 1540

commit v2 on v1

--- a/solution.py
+++ b/solution.py
@@ -12,13 +12,12 @@
 NA = 4
 F32, BF16 = jnp.float32, jnp.bfloat16
 SENDS = 160
-FAR_GREETING = True
 
 
 def body(
     resid, target, enc, bias, dec, blocks,
     x_out, low_out, bias_out, err_out,
-    X, XO, XS, WE, BI, DW, TG, PP, PR, S0, S1, R0, R1, B0, B1, Q0, Q1,
+    X, XO, XO_T, XS_T, WE, BI, DW, TG, PP, PR, S0, S1, R0, R1, B0, B1, Q0, Q1,
     S2, S2F, R2, YO, YA, YN, YB, E, EM, GP, GR, loc, ssem, rsem,
 ):
     y, h = lax.axis_index("y"), lax.axis_index("core")
@@ -37,9 +36,8 @@
     sibling = {"core": other}
 
     barrier = pltpu.get_barrier_semaphore()
-    near = [sibling, at_x(1), at_x(2), at_x(3), at_z(1), at_z(-1)]
-    if FAR_GREETING:
-        near += [at_z(d) for d in (2, -2, 4, -4, 8)]
+    near = [sibling, at_x(1), at_x(2), at_x(3)]
+    near += [at_z(d) for d in (1, -1, 2, -2, 3, -3, 4, -4)]
     for peer in near:
         pl.semaphore_signal(barrier, inc=1, device_id=peer, device_id_type=pl.DeviceIdType.MESH)
 
@@ -89,27 +87,38 @@
         zz = lax.rem(z + d + NZ, NZ)
         return lax.rem(zz, 4), lax.div(zz, 4)
 
-    up = send(mine, X.at[r, x, a], at_z(1))
-    down = send(mine, X.at[r, x, a], at_z(-1))
-    across = [send(mine, X.at[r, x, a], at_x(d)) for d in (2, 1, 3)]
+    def gathered(buf, src):
+        own = buf.at[r, x, a]
+        out = {d: send(src, own, at_z(d)) for d in (4, -4, 3, -3, 2, -2, 1, -1)}
+        across = [send(src, own, at_x(d)) for d in (2, 1, 3)]
+
+        def passed(d):
+            rr, aa = slot(-d)
+            got = buf.at[rr, x, aa]
+            return got, [send(got, got, at_x(dx)) for dx in (2, 1, 3)]
+
+        for d in (1, -1, 2, -2, 3, -3):
+            out[d].wait_recv()
+            across += passed(d)[1]
+        far = {}
+        for d, steps in ((4, (4, 3, 2, 1)), (-4, (-3, -2, -1))):
+            out[d].wait_recv()
+            rr, aa = slot(-d)
+            got = buf.at[rr, x, aa]
+            for k in steps:
+                far[k + d] = send(got, got, at_z(k))
+        for d in (4, -4):
+            across += passed(d)[1]
+        for d in (5, -5, 6, -6, 7, -7, 8):
+            far[d].wait_recv()
+            across += passed(d)[1]
+        return across
+
     enc_far = send(
         enc.at[0, pl.ds(pl.multiple_of(other * half, 128), half), :],
         WE.at[:, pl.ds(pl.multiple_of(h * width, 128), width)], sibling)
     bias_far = send(bias, BI.at[h], sibling)
-    for s in range(1, 9):
-        up.wait_recv()
-        rr, aa = slot(-s)
-        got = X.at[rr, x, aa]
-        if s < 8:
-            up = send(got, got, at_z(1))
-        across += [send(got, got, at_x(d)) for d in (2, 1, 3)]
-        if s < 8:
-            down.wait_recv()
-            rr, aa = slot(s)
-            got = X.at[rr, x, aa]
-            if s < 7:
-                down = send(got, got, at_z(-1))
-            across += [send(got, got, at_x(d)) for d in (2, 1, 3)]
+    across = gathered(X, mine)
 
     row = blocks[y]
     column = x * NZ + z
@@ -128,12 +137,10 @@
     keep.wait()
     for copy in across:
         copy.wait_recv()
-    rows = 4 * NX * NA * 2
     for rr in range(4):
         XO[pl.ds(rr * 32, 32), :] = X[rr].reshape(32, half)
     PP[...] = jnp.dot(XO[...], WE[...], preferred_element_type=F32)
     part = send(PP, PR, sibling)
-    rows_far = send(XO, XS, sibling)
     part.wait_recv()
     biases = jnp.concatenate([BI[0], BI[1]], axis=1)
     acts = ((PP[...] + PR[...] + biases) * gates).astype(BF16)
@@ -158,6 +165,9 @@
                 send(S0.at[:, lax.rem(x + d, NX)], R0.at[i], at_x(d))
                 for i, d in enumerate((2, 1, 3))
             ]
+    for n in range(0, half, step):
+        XO_T[n:n + step, :] = XO[:, n:n + step].T
+    rows_far = send(XO_T, XS_T, sibling)
     for copy in in1:
         copy.wait_recv()
 
@@ -232,46 +242,21 @@
     err_own = (sums[0] + YB[...] - TG[0].astype(F32)).astype(BF16)
     err_next = (YN[...] + sums[1] - TG[1].astype(F32)).astype(BF16)
     err_out[0] = err_own
-    E[0, r, x, a] = err_own
-    E[1, r, x, a] = err_next
-
-    piece = E.at[:, r, x, a]
-    gathered = [send(piece, piece, at_z(d)) for d in (8, 4, -4)]
-    for copy in gathered:
-        copy.wait_recv()
-    h2 = NA // 2
-
-    def along_x(t, rr):
-        block = E.at[t, rr, x]
-        return [send(block, block, at_x(d)) for d in (2, 1, 3)]
-
-    def along_z(t, xx):
-        lo, hi = E.at[t, r, xx, pl.ds(0, h2)], E.at[t, r, xx, pl.ds(h2, h2)]
-        block = E.at[t, r, xx]
-        return [
-            send(lo, lo, at_z(-2)), send(hi, hi, at_z(2)),
-            send(block, block, at_z(-1)), send(block, block, at_z(1)),
-        ]
-
-    first0 = along_z(0, x)
-    first1 = along_x(1, r)
-    rest = along_x(0, r) + along_z(1, x)
-    for d, copy in zip((2, 1, 3), first1):
-        copy.wait_recv()
-        rest += along_z(1, lax.rem(x + NX - d, NX))
-    first0[2].wait_recv()
-    rest += along_x(0, r1)
-    first0[3].wait_recv()
-    rest += along_x(0, r3)
-    first0[0].wait_recv()
-    first0[1].wait_recv()
-    rest += along_x(0, r2)
-    for copy in rest:
+    E[r, x, a, 0] = err_own
+    E[r, x, a, 1] = err_next
+
+    rows_far.wait_recv()
+    out_a = pltpu.make_async_copy(XO_T, x_out.at[h], loc.at[5])
+    out_b = pltpu.make_async_copy(XS_T, x_out.at[other], loc.at[6])
+    out_a.start()
+    out_b.start()
+
+    for copy in gathered(E, E.at[r, x, a]):
         copy.wait_recv()
     grad = None
     for t in range(2):
         for rr in range(4):
-            EM[pl.ds(rr * 32, 32), :] = E[t, rr].reshape(32, half)
+            EM[pl.ds(rr * 32, 32), :] = E[rr, :, :, t].reshape(32, half)
         term = lax.dot_general(
             EM[...], DW[t].reshape(2 * width, half), (((1,), (1,)), ((), ())),
             preferred_element_type=F32)
@@ -280,11 +265,6 @@
     GP[1] = grad[:, width:]
     back = send(GP.at[other], GR, sibling)
 
-    rows_far.wait_recv()
-    out_a = pltpu.make_async_copy(XO, x_out.at[h], loc.at[5])
-    out_b = pltpu.make_async_copy(XS, x_out.at[other], loc.at[6])
-    out_a.start()
-    out_b.start()
     back.wait_recv()
     grad_pre = (GP[h] + GR[...]) * gate_own
     bias_out[...] = jnp.sum(grad_pre, axis=0, keepdims=True)
@@ -314,7 +294,7 @@
     x_all, low, bias_grad, errors = pl.pallas_call(
         body,
         out_shape=(
-            jax.ShapeDtypeStruct((2, rows, half), BF16),
+            jax.ShapeDtypeStruct((2, half, rows), BF16),
             jax.ShapeDtypeStruct((rows, width), BF16),
             jax.ShapeDtypeStruct((1, width), F32),
             jax.ShapeDtypeStruct((1, 2, half), BF16),
@@ -324,7 +304,8 @@
         scratch_shapes=[
             V((4, NX, NA, 2, half), BF16),
             V((rows, half), BF16),
-            V((rows, half), BF16),
+            V((half, rows), BF16),
+            V((half, rows), BF16),
             V((half, 2 * width), BF16),
             V((2, 1, width), F32),
             V((2, 2, width, half), BF16),
@@ -346,7 +327,7 @@
             V((2, half), F32),
             V((2, half), F32),
             V((2, half), F32),
-            V((2, 4, NX, NA, 2, half), BF16),
+            V((4, NX, NA, 2, 2, half), BF16),
             V((rows, half), BF16),
             V((2, rows, width), F32),
             V((rows, width), F32),
@@ -357,9 +338,39 @@
         compiler_params=pltpu.CompilerParams(collective_id=0, has_side_effects=True),
         name="step",
     )(resid, target, enc, bias, dec, blocks)
-    grad = lax.dot_general(
-        x_all, low, (((1,), (0,)), ((), ())), preferred_element_type=F32)
-    return errors, grad.astype(BF16).reshape(1, 2 * half, width), bias_grad
+    parts = 4
+    tall = 2 * half // parts
+    grad, bias_grad, errors = pl.pallas_call(
+        weight_gradient,
+        grid=(parts,),
+        out_shape=(
+            jax.ShapeDtypeStruct((1, 2 * half, width), BF16),
+            jax.ShapeDtypeStruct((1, width), F32),
+            jax.ShapeDtypeStruct((1, 2, half), BF16),
+        ),
+        in_specs=[
+            pl.BlockSpec((tall, rows), lambda i: (i, 0)),
+            pl.BlockSpec((rows, width), lambda i: (0, 0)),
+            pl.BlockSpec((1, width), lambda i: (0, 0)),
+            pl.BlockSpec((1, 2, half), lambda i: (0, 0, 0)),
+        ],
+        out_specs=(
+            pl.BlockSpec((1, tall, width), lambda i: (0, i, 0)),
+            pl.BlockSpec((1, width), lambda i: (0, 0)),
+            pl.BlockSpec((1, 2, half), lambda i: (0, 0, 0)),
+        ),
+        name="weights",
+    )(x_all.reshape(2 * half, rows), low, bias_grad, errors)
+    return errors, grad, bias_grad
+
+
+def weight_gradient(xt, low, bias_in, err_in, grad, bias_out, err_out):
+    grad[0] = jnp.dot(xt[...], low[...], preferred_element_type=F32).astype(BF16)
+
+    @pl.when(pl.program_id(0) == 0)
+    def _():
+        bias_out[...] = bias_in[...]
+        err_out[...] = err_in[...]
 
 
 def solution(mesh):

time: 92.4 us -> 76.3 us (0.83)
  Pallas kernels: 88 us -> 75.4 us
  matrix products: 2.54 us -> 0 us
  local copies, waits for them, and re-layouts: 1.11 us -> 0 us
    pallas_call x1 -> x2, Pallas kernels: 88 us -> 75.4 us  [the longest x1 71.7 us: on_device(): pl.pallas_call(body, out_shape=(jax.ShapeDtypeStruct((2, half, rows), BF1...]
    dot_general x1 -> x0, matrix products: 2.54 us -> none  [on_device(): lax.dot_general(x_all, low, (((1,), (0,)), ((), ())), preferred_element_t...]
    unnamed x6 -> x0, local copies, waits for them, and re-layouts: 1.11 us -> none
where the time goes in v2:
time: 76.3 us; the launch traced here: 76 us
  Pallas kernels  75.4 us (99%)
    pallas_call x1, Pallas kernels, on_device(): pl.pallas_call(body, out_shape=(jax.ShapeDtypeStruct((2, half, rows), BF1...  71.7 us
    pallas_call x1, Pallas kernels, on_device(): pl.pallas_call(weight_gradient, grid=(parts,), out_shape=(jax.ShapeDtypeS...  3.71 us

profile of v2, /device:TPU:1, one launch (start us, length us, event | category | flops | bytes accessed | tf_op | source)
XLA Modules:
  0.0 76.0 jit_solution(16170565929302833234)
XLA Ops:
  0.6 71.7 %step.1 = (bf16[2,1792,128]{2,1,0:T(8,128)(2,1)}, bf16[128,128]{1,0:T(8,128)(2,1)}, f32[1,128]{1,0:T(1,128)}, bf16[1,2,1792]{2,1,0:T(2,128)(2,1)}) custom-call(bf16[4,2,3584]{2,1,0:T(2,128)(2,1)} %resid.1, bf16[5,2,3584]{2,1,0:T(2,128)(2,1)} %target.1, bf16[1,3584,128]{2,1,0:T(8,128)(2,1)} %enc.1, f32[1,128]{1,0:T(1,128)} %bias.1, ...), custom_call_target="tpu_custom_call" | custom-call | tf_op jit(solution)/shard_map/step/pallas_call | solution.py:294
  72.3 3.7 %weights.1 = (bf16[1,3584,128]{2,1,0:T(8,128)(2,1)}, f32[1,128]{1,0:T(1,128)}, bf16[1,2,1792]{2,1,0:T(2,128)(2,1)}) custom-call(bf16[3584,128]{1,0:T(8,128)(2,1)} %bitcast.1, bf16[128,128]{1,0:T(8,128)(2,1)} %get-tuple-element.11.low, f32[1,128]{1,0:T(1,128)} %get-tuple-element.12.bias_in, bf16[1,2,1792]{2,1,0:T(2,128)(2,1)} %get-tuple-element.13.err_in), custom_call_target="tpu_custom_call" | custom-call | tf_op jit(solution)/shard_map/weights/pallas_call | solution.py:343

commit v3 on v2

--- a/solution.py
+++ b/solution.py
@@ -11,7 +11,8 @@
 NY, NX, NZ = 4, 4, 16
 NA = 4
 F32, BF16 = jnp.float32, jnp.bfloat16
-SENDS = 160
+SENDS = 184
+PARTS = 7
 
 
 def body(
@@ -147,29 +148,34 @@
 
     dec_in.wait()
     step = 256
+    n2 = half // 2
+    lo, hi = pl.ds(0, n2), pl.ds(n2, n2)
+    r1, r3, r2 = lax.rem(r + 1, 4), lax.rem(r + 3, 4), lax.rem(r + 2, 4)
+    classes = ((2, r2), (1, r1), (3, r3), (0, r))
+    in1, in0 = {}, {}
     for t, S in ((1, S1), (0, S0)):
         for n in range(0, half, step):
             w = DW[t, :, :, n:n + step].reshape(2 * width, step)
             p = jnp.dot(acts, w, preferred_element_type=F32)
             S[:, :, :, n:n + step] = p.reshape(4, NX, 8, step).astype(BF16)
         if t == 1:
-            r1, r3, r2 = lax.rem(r + 1, 4), lax.rem(r + 3, 4), lax.rem(r + 2, 4)
-            in1 = [
-                send(S1.at[r2, pl.ds(0, 2)], R1.at[2, pl.ds(0, 2)], at_z(2)),
-                send(S1.at[r2, pl.ds(2, 2)], R1.at[2, pl.ds(2, 2)], at_z(-2)),
-                send(S1.at[r1], R1.at[0], at_z(1)),
-                send(S1.at[r3], R1.at[1], at_z(-1)),
-            ]
+            for d in (2, 1, 3, 0):
+                xx = lax.rem(x + d, NX)
+                in1[d] = [
+                    send(S1.at[r2, xx, :, lo], R1.at[2, xx, :, lo], at_z(2)),
+                    send(S1.at[r2, xx, :, hi], R1.at[2, xx, :, hi], at_z(-2)),
+                    send(S1.at[r1, xx], R1.at[0, xx], at_z(1)),
+                    send(S1.at[r3, xx], R1.at[1, xx], at_z(-1)),
+                ]
         else:
-            in0 = [
-                send(S0.at[:, lax.rem(x + d, NX)], R0.at[i], at_x(d))
-                for i, d in enumerate((2, 1, 3))
-            ]
+            for d, rr in classes:
+                in0[d] = [
+                    send(S0.at[rr, lax.rem(x + dx, NX)], R0.at[i, rr], at_x(dx))
+                    for i, dx in enumerate((2, 1, 3))
+                ]
     for n in range(0, half, step):
         XO_T[n:n + step, :] = XO[:, n:n + step].T
     rows_far = send(XO_T, XS_T, sibling)
-    for copy in in1:
-        copy.wait_recv()
 
     def summed1(xx):
         return (S1[r, xx].astype(F32) + R1[0, xx].astype(F32)) + (
@@ -179,25 +185,27 @@
         return (S0[rr, x].astype(F32) + R0[0, rr].astype(F32)) + (
             R0[1, rr].astype(F32) + R0[2, rr].astype(F32))
 
-    next1 = []
-    for i, d in enumerate((2, 1, 3)):
+    def landed(copies):
+        for copy in copies:
+            copy.wait_recv()
+
+    after = []
+    for i, (d, rr) in enumerate(classes[:3]):
+        landed(in1[d])
         B1[i] = summed1(lax.rem(x + d, NX)).astype(BF16)
-        next1.append(send(B1.at[i], Q1.at[i], at_x(d)))
-    for copy in in0:
-        copy.wait_recv()
-    next0 = []
-    n2 = half // 2
-    B0[2] = summed0(r2).astype(BF16)
-    next0.append(send(B0.at[2, :, pl.ds(0, n2)], Q0.at[2, :, pl.ds(0, n2)], at_z(2)))
-    next0.append(send(B0.at[2, :, pl.ds(n2, n2)], Q0.at[2, :, pl.ds(n2, n2)], at_z(-2)))
-    B0[0] = summed0(r1).astype(BF16)
-    next0.append(send(B0.at[0], Q0.at[0], at_z(1)))
-    B0[1] = summed0(r3).astype(BF16)
-    next0.append(send(B0.at[1], Q0.at[1], at_z(-1)))
+        after.append(send(B1.at[i], Q1.at[i], at_x(d)))
+        landed(in0[d])
+        B0[i] = summed0(rr).astype(BF16)
+        if d == 2:
+            after.append(send(B0.at[i, :, lo], Q0.at[i, :, lo], at_z(2)))
+            after.append(send(B0.at[i, :, hi], Q0.at[i, :, hi], at_z(-2)))
+        else:
+            after.append(send(B0.at[i], Q0.at[i], at_z(1 if d == 1 else -1)))
+    landed(in1[0])
     own1 = summed1(x)
+    landed(in0[0])
     own0 = summed0(r)
-    for copy in next1 + next0:
-        copy.wait_recv()
+    landed(after)
     for t, own, Q in ((0, own0, Q0), (1, own1, Q1)):
         total = (own + Q[0].astype(F32)) + (Q[1].astype(F32) + Q[2].astype(F32))
         for aa in range(NA):
@@ -288,7 +296,7 @@
     half = dec.shape[-1]
     width = enc.shape[-1]
     rows = 128
-    any_spec = pl.BlockSpec(memory_space=pl.ANY)
+    hbm = pl.BlockSpec(memory_space=pltpu.HBM)
     vmem = pl.BlockSpec(memory_space=pltpu.VMEM)
     V = pltpu.VMEM
     x_all, low, bias_grad, errors = pl.pallas_call(
@@ -299,8 +307,8 @@
             jax.ShapeDtypeStruct((1, width), F32),
             jax.ShapeDtypeStruct((1, 2, half), BF16),
         ),
-        in_specs=[any_spec] * 5 + [vmem],
-        out_specs=(any_spec, vmem, vmem, vmem),
+        in_specs=[hbm] * 5 + [vmem],
+        out_specs=(vmem,) * 4,
         scratch_shapes=[
             V((4, NX, NA, 2, half), BF16),
             V((rows, half), BF16),
@@ -335,42 +343,40 @@
             pltpu.SemaphoreType.DMA((SENDS,)),
             pltpu.SemaphoreType.DMA((SENDS,)),
         ],
-        compiler_params=pltpu.CompilerParams(collective_id=0, has_side_effects=True),
+        compiler_params=pltpu.CompilerParams(
+            collective_id=0, has_side_effects=True, vmem_limit_bytes=53700 << 10),
         name="step",
     )(resid, target, enc, bias, dec, blocks)
-    parts = 4
-    tall = 2 * half // parts
+    tall = 2 * half // PARTS
     grad, bias_grad, errors = pl.pallas_call(
         weight_gradient,
-        grid=(parts,),
         out_shape=(
             jax.ShapeDtypeStruct((1, 2 * half, width), BF16),
             jax.ShapeDtypeStruct((1, width), F32),
             jax.ShapeDtypeStruct((1, 2, half), BF16),
         ),
-        in_specs=[
-            pl.BlockSpec((tall, rows), lambda i: (i, 0)),
-            pl.BlockSpec((rows, width), lambda i: (0, 0)),
-            pl.BlockSpec((1, width), lambda i: (0, 0)),
-            pl.BlockSpec((1, 2, half), lambda i: (0, 0, 0)),
-        ],
-        out_specs=(
-            pl.BlockSpec((1, tall, width), lambda i: (0, i, 0)),
-            pl.BlockSpec((1, width), lambda i: (0, 0)),
-            pl.BlockSpec((1, 2, half), lambda i: (0, 0, 0)),
-        ),
+        in_specs=[vmem] * 4,
+        out_specs=(hbm, vmem, vmem),
+        scratch_shapes=[V((PARTS, tall, width), BF16), pltpu.SemaphoreType.DMA((PARTS,))],
+        compiler_params=pltpu.CompilerParams(vmem_limit_bytes=8 << 20),
         name="weights",
     )(x_all.reshape(2 * half, rows), low, bias_grad, errors)
     return errors, grad, bias_grad
 
 
-def weight_gradient(xt, low, bias_in, err_in, grad, bias_out, err_out):
-    grad[0] = jnp.dot(xt[...], low[...], preferred_element_type=F32).astype(BF16)
-
-    @pl.when(pl.program_id(0) == 0)
-    def _():
-        bias_out[...] = bias_in[...]
-        err_out[...] = err_in[...]
+def weight_gradient(xt, low, bias_in, err_in, grad, bias_out, err_out, held, sems):
+    tall = held.shape[1]
+    copies = []
+    for i in range(PARTS):
+        part = jnp.dot(xt[i * tall:(i + 1) * tall, :], low[...], preferred_element_type=F32)
+        held[i] = part.astype(BF16)
+        copies.append(pltpu.make_async_copy(
+            held.at[i], grad.at[0, pl.ds(i * tall, tall), :], sems.at[i]))
+        copies[-1].start()
+    bias_out[...] = bias_in[...]
+    err_out[...] = err_in[...]
+    for copy in copies:
+        copy.wait()
 
 
 def solution(mesh):

time: 76.3 us -> 75.2 us (0.986)
  Pallas kernels: 75.4 us -> 71.2 us
  local copies, waits for them, and re-layouts: 0 us -> 3.03 us
    unnamed x0 -> x8, local copies, waits for them, and re-layouts: none -> 3.03 us
    pallas_call x1, Pallas kernels: 71.7 us -> 69.5 us  [on_device(): pl.pallas_call(body, out_shape=(jax.ShapeDtypeStruct((2, half, rows), BF1...]
    pallas_call x1, Pallas kernels: 3.71 us -> 1.78 us  [on_device(): pl.pallas_call(weight_gradient, out_shape=(jax.ShapeDtypeStruct((1, 2 * h...]
where the time goes in v3:
time: 75.2 us; the launch traced here: 74.9 us
  Pallas kernels  71.2 us (95%)
  local copies, waits for them, and re-layouts  3.03 us (4%)
    pallas_call x1, Pallas kernels, on_device(): pl.pallas_call(body, out_shape=(jax.ShapeDtypeStruct((2, half, rows), BF1...  69.5 us
    unnamed x8, local copies, waits for them, and re-layouts  3.03 us
    pallas_call x1, Pallas kernels, on_device(): pl.pallas_call(weight_gradient, out_shape=(jax.ShapeDtypeStruct((1, 2 * h...  1.78 us

profile of v3, /device:TPU:1, one launch (start us, length us, event | category | flops | bytes accessed | tf_op | source)
XLA Modules:
  0.0 74.9 jit_solution(339268516149475525)
XLA Ops:
  0.6 0.0 copy-start
  0.6 0.9 %copy-done = bf16[5,2,3584]{2,1,0:T(2,128)(2,1)S(1)} copy-done((bf16[5,2,3584]{2,1,0:T(2,128)(2,1)S(1)}, bf16[5,2,3584]{2,1,0:T(2,128)(2,1)}, u32[]{:S(2)}) %copy-start) | copy-done | bytes 71704
  1.5 0.0 copy-start.1
  1.5 0.8 %copy-done.1 = bf16[4,2,3584]{2,1,0:T(2,128)(2,1)S(1)} copy-done((bf16[4,2,3584]{2,1,0:T(2,128)(2,1)S(1)}, bf16[4,2,3584]{2,1,0:T(2,128)(2,1)}, u32[]{:S(2)}) %copy-start.1) | copy-done | bytes 57368
  2.3 0.0 copy-start.2
  2.3 0.7 copy-done.2
  3.0 0.0 copy-start.3
  3.0 0.7 copy-done.3
  3.7 69.5 %step.1 = (bf16[2,1792,128]{2,1,0:T(8,128)(2,1)S(1)}, bf16[128,128]{1,0:T(8,128)(2,1)S(1)}, f32[1,128]{1,0:T(1,128)S(1)}, bf16[1,2,1792]{2,1,0:T(2,128)(2,1)S(1)}) custom-call(bf16[4,2,3584]{2,1,0:T(2,128)(2,1)S(1)} %copy-done.1, bf16[5,2,3584]{2,1,0:T(2,128)(2,1)S(1)} %copy-done, bf16[1,3584,128]{2,1,0:T(8,128)(2,1)} %enc.1, f32[1,128]{1,0:T(1,128)S(1)} %copy-done.3, ...), custom_call_target="tpu_custom_call" | custom-call | tf_op jit(solution)/shard_map/step/pallas_call | solution.py:302
  73.1 1.8 %weights.1 = (bf16[1,3584,128]{2,1,0:T(8,128)(2,1)}, f32[1,128]{1,0:T(1,128)}, bf16[1,2,1792]{2,1,0:T(2,128)(2,1)}) custom-call(bf16[3584,128]{1,0:T(8,128)(2,1)S(1)} %bitcast.1, bf16[128,128]{1,0:T(8,128)(2,1)S(1)} %get-tuple-element.11.low, f32[1,128]{1,0:T(1,128)S(1)} %get-tuple-element.12.bias_in, bf16[1,2,1792]{2,1,0:T(2,128)(2,1)S(1)} %get-tuple-element.13.err_in), custom_call_target="tpu_custom_call" | custom-call | tf_op jit(solution)/shard_map/weights/pallas_call | solution.py:351
Async XLA Ops:
  0.6 0.9 %copy-start = (bf16[5,2,3584]{2,1,0:T(2,128)(2,1)S(1)}, bf16[5,2,3584]{2,1,0:T(2,128)(2,1)}, u32[]{:S(2)}) copy-start(bf16[5,2,3584]{2,1,0:T(2,128)(2,1)} %target.1) | copy-start | bytes 215044
  1.5 0.8 %copy-start.1 = (bf16[4,2,3584]{2,1,0:T(2,128)(2,1)S(1)}, bf16[4,2,3584]{2,1,0:T(2,128)(2,1)}, u32[]{:S(2)}) copy-start(bf16[4,2,3584]{2,1,0:T(2,128)(2,1)} %resid.1) | copy-start | bytes 172036
  2.3 0.7 copy-start.2
  3.0 0.7 copy-start.3

commit v4 on v3

--- a/solution.py
+++ b/solution.py
@@ -11,7 +11,7 @@
 NY, NX, NZ = 4, 4, 16
 NA = 4
 F32, BF16 = jnp.float32, jnp.bfloat16
-SENDS = 184
+SENDS = 200
 PARTS = 7
 
 
@@ -19,7 +19,7 @@
     resid, target, enc, bias, dec, blocks,
     x_out, low_out, bias_out, err_out,
     X, XO, XO_T, XS_T, WE, BI, DW, TG, PP, PR, S0, S1, R0, R1, B0, B1, Q0, Q1,
-    S2, S2F, R2, YO, YA, YN, YB, E, EM, GP, GR, loc, ssem, rsem,
+    S2, S2F, R2, YO, YA, YN, YB, E, EM, GP, GR, BK, loc, ssem, rsem,
 ):
     y, h = lax.axis_index("y"), lax.axis_index("core")
     x, z = lax.axis_index("x"), lax.axis_index("z")
@@ -65,6 +65,8 @@
     dec_in = pltpu.make_async_copy(dec.at[0], DW, loc.at[4])
     dec_in.start()
 
+    fire = pltpu.make_async_copy(blocks, BK, loc.at[7])
+    fire.start()
     extra = jnp.where(jnp.logical_and(y > 0, y < NY - 1), 2, 1)
     pl.semaphore_wait(barrier, len(near) + extra)
 
@@ -115,13 +117,79 @@
             across += passed(d)[1]
         return across
 
+    def gathered_pairs(buf):
+        own = buf.at[r, x, a]
+        out = {d: send(own, own, at_z(d)) for d in (4, -4, 3, -3, 2, -2, 1, -1)}
+        left, right = lax.rem(x + 3, NX), lax.rem(x + 1, NX)
+        beside = {}
+        rest = []
+
+        def to_sides(d):
+            rr, aa = slot(-d)
+            got = buf.at[rr, x, aa]
+            beside[d] = (send(got, got, at_x(1)), send(got, got, at_x(3)))
+
+        def relayed(d):
+            rr, aa = slot(-d)
+            beside[d][0].wait_recv()
+            first = buf.at[rr, left, aa, 0]
+            beside[d][1].wait_recv()
+            second = buf.at[rr, right, aa, 1]
+            return [send(first, first, at_x(1)), send(second, second, at_x(3))]
+
+        def to_next(xx):
+            got = buf.at[r, xx, a]
+            return [send(got, got, at_z(d)) for d in (1, -1)]
+
+        def to_all(d):
+            far[d].wait_recv()
+            rr, aa = slot(-d)
+            got = buf.at[rr, x, aa]
+            return [send(got, got, at_x(dx)) for dx in (2, 1, 3)]
+
+        to_sides(0)
+        for d in (2, -2):
+            out[d].wait_recv()
+            to_sides(d)
+        opposite = relayed(0)
+        rest += to_next(left) + to_next(right)
+        far = {}
+        for d, steps in ((4, (4, 3, 2, 1)), (-4, (-3, -2, -1))):
+            out[d].wait_recv()
+            rr, aa = slot(-d)
+            got = buf.at[rr, x, aa]
+            for k in steps:
+                far[k + d] = send(got, got, at_z(k))
+        for d in (3, -3):
+            out[d].wait_recv()
+            to_sides(d)
+        for d in (4, -4):
+            to_sides(d)
+        for d in (2, -2):
+            rest += relayed(d)
+        for copy in opposite:
+            copy.wait_recv()
+        rest += to_next(lax.rem(x + 2, NX))
+        for d in (5, -5):
+            rest += to_all(d)
+        for d in (3, -3):
+            rest += relayed(d)
+        for d in (6, -6):
+            rest += to_all(d)
+        for d in (4, -4):
+            rest += relayed(d)
+        for d in (7, -7, 8):
+            rest += to_all(d)
+        return rest + [out[1], out[-1]]
+
     enc_far = send(
         enc.at[0, pl.ds(pl.multiple_of(other * half, 128), half), :],
         WE.at[:, pl.ds(pl.multiple_of(h * width, 128), width)], sibling)
     bias_far = send(bias, BI.at[h], sibling)
     across = gathered(X, mine)
 
-    row = blocks[y]
+    fire.wait()
+    row = BK[y]
     column = x * NZ + z
     hits = [
         jnp.max((row == g * NX * NZ + column).astype(F32), axis=1, keepdims=True)
@@ -259,22 +327,25 @@
     out_a.start()
     out_b.start()
 
-    for copy in gathered(E, E.at[r, x, a]):
+    for copy in gathered_pairs(E):
         copy.wait_recv()
-    grad = None
     for t in range(2):
         for rr in range(4):
-            EM[pl.ds(rr * 32, 32), :] = E[rr, :, :, t].reshape(32, half)
-        term = lax.dot_general(
-            EM[...], DW[t].reshape(2 * width, half), (((1,), (1,)), ((), ())),
-            preferred_element_type=F32)
-        grad = term if grad is None else grad + term
-    GP[0] = grad[:, :width]
-    GP[1] = grad[:, width:]
-    back = send(GP.at[other], GR, sibling)
-
+            EM[t, pl.ds(rr * 32, 32), :] = E[rr, :, :, t].reshape(32, half)
+
+    def latent_grad(g):
+        terms = [
+            lax.dot_general(
+                EM[t], DW[t, g], (((1,), (1,)), ((), ())), preferred_element_type=F32)
+            for t in range(2)
+        ]
+        return terms[0] + terms[1]
+
+    GP[...] = latent_grad(other)
+    back = send(GP, GR, sibling)
+    grad_own = latent_grad(h)
     back.wait_recv()
-    grad_pre = (GP[h] + GR[...]) * gate_own
+    grad_pre = (grad_own + GR[...]) * gate_own
     bias_out[...] = jnp.sum(grad_pre, axis=0, keepdims=True)
     low_out[...] = grad_pre.astype(BF16)
     for copy in started:
@@ -299,6 +370,9 @@
     hbm = pl.BlockSpec(memory_space=pltpu.HBM)
     vmem = pl.BlockSpec(memory_space=pltpu.VMEM)
     V = pltpu.VMEM
+    resid, target, enc, bias, dec, blocks = (
+        pltpu.with_memory_space_constraint(v, pltpu.HBM)
+        for v in (resid, target, enc, bias, dec, blocks))
     x_all, low, bias_grad, errors = pl.pallas_call(
         body,
         out_shape=(
@@ -307,7 +381,7 @@
             jax.ShapeDtypeStruct((1, width), F32),
             jax.ShapeDtypeStruct((1, 2, half), BF16),
         ),
-        in_specs=[hbm] * 5 + [vmem],
+        in_specs=[hbm] * 6,
         out_specs=(vmem,) * 4,
         scratch_shapes=[
             V((4, NX, NA, 2, half), BF16),
@@ -336,9 +410,10 @@
             V((2, half), F32),
             V((2, half), F32),
             V((4, NX, NA, 2, 2, half), BF16),
-            V((rows, half), BF16),
-            V((2, rows, width), F32),
+            V((2, rows, half), BF16),
             V((rows, width), F32),
+            V((rows, width), F32),
+            V(blocks.shape, jnp.int32),
             pltpu.SemaphoreType.DMA((8,)),
             pltpu.SemaphoreType.DMA((SENDS,)),
             pltpu.SemaphoreType.DMA((SENDS,)),

time: 75.2 us -> 72.4 us (0.963)
  local copies, waits for them, and re-layouts: 3.03 us -> 0 us
    unnamed x8 -> x0, local copies, waits for them, and re-layouts: 3.03 us -> none
where the time goes in v4:
time: 72.4 us; the launch traced here: 72.3 us
  Pallas kernels  71.6 us (99%)
    pallas_call x1, Pallas kernels, on_device(): pl.pallas_call(body, out_shape=(jax.ShapeDtypeStruct((2, half, rows), BF1...  69.8 us
    pallas_call x1, Pallas kernels, on_device(): pl.pallas_call(weight_gradient, out_shape=(jax.ShapeDtypeStruct((1, 2 * h...  1.78 us

profile of v4, /device:TPU:1, one launch (start us, length us, event | category | flops | bytes accessed | tf_op | source)
XLA Modules:
  0.0 72.3 jit_solution(1912924434958477895)
XLA Ops:
  0.6 69.8 %step.1 = (bf16[2,1792,128]{2,1,0:T(8,128)(2,1)S(1)}, bf16[128,128]{1,0:T(8,128)(2,1)S(1)}, f32[1,128]{1,0:T(1,128)S(1)}, bf16[1,2,1792]{2,1,0:T(2,128)(2,1)S(1)}) custom-call(bf16[4,2,3584]{2,1,0:T(2,128)(2,1)} %resid.1, bf16[5,2,3584]{2,1,0:T(2,128)(2,1)} %target.1, bf16[1,3584,128]{2,1,0:T(8,128)(2,1)} %enc.1, f32[1,128]{1,0:T(1,128)} %bias.1, ...), custom_call_target="tpu_custom_call" | custom-call | tf_op jit(solution)/shard_map/step/pallas_call | solution.py:376
  70.5 1.8 %weights.1 = (bf16[1,3584,128]{2,1,0:T(8,128)(2,1)}, f32[1,128]{1,0:T(1,128)}, bf16[1,2,1792]{2,1,0:T(2,128)(2,1)}) custom-call(bf16[3584,128]{1,0:T(8,128)(2,1)S(1)} %bitcast.1, bf16[128,128]{1,0:T(8,128)(2,1)S(1)} %get-tuple-element.11.low, f32[1,128]{1,0:T(1,128)S(1)} %get-tuple-element.12.bias_in, bf16[1,2,1792]{2,1,0:T(2,128)(2,1)S(1)} %get-tuple-element.13.err_in), custom_call_target="tpu_custom_call" | custom-call | tf_op jit(solution)/shard_map/weights/pallas_call | solution.py:426

commit v5 on v3

--- a/solution.py
+++ b/solution.py
@@ -11,7 +11,7 @@
 NY, NX, NZ = 4, 4, 16
 NA = 4
 F32, BF16 = jnp.float32, jnp.bfloat16
-SENDS = 184
+SENDS = 216
 PARTS = 7
 
 
@@ -19,7 +19,7 @@
     resid, target, enc, bias, dec, blocks,
     x_out, low_out, bias_out, err_out,
     X, XO, XO_T, XS_T, WE, BI, DW, TG, PP, PR, S0, S1, R0, R1, B0, B1, Q0, Q1,
-    S2, S2F, R2, YO, YA, YN, YB, E, EM, GP, GR, loc, ssem, rsem,
+    S2, S2F, R2, QN, QB, E, EM, GP, GR, BK, loc, ssem, rsem,
 ):
     y, h = lax.axis_index("y"), lax.axis_index("core")
     x, z = lax.axis_index("x"), lax.axis_index("z")
@@ -42,13 +42,26 @@
     for peer in near:
         pl.semaphore_signal(barrier, inc=1, device_id=peer, device_id_type=pl.DeviceIdType.MESH)
 
+    def greet(peers):
+        for peer in peers:
+            pl.semaphore_signal(
+                barrier, inc=1, device_id=peer, device_id_type=pl.DeviceIdType.MESH)
+
     @pl.when(y > 0)
     def _():
-        pl.semaphore_signal(barrier, inc=1, device_id={"y": y - 1}, device_id_type=pl.DeviceIdType.MESH)
+        greet([{"y": y - 1}] + [{"y": y - 1, **at_x(d)} for d in (1, 2, 3)])
 
     @pl.when(y < NY - 1)
     def _():
-        pl.semaphore_signal(barrier, inc=1, device_id={"y": y + 1}, device_id_type=pl.DeviceIdType.MESH)
+        greet([{"y": y + 1}] + [{"y": y + 1, **at_z(d)} for d in (1, -1, 2, -2)])
+
+    @pl.when(y == 0)
+    def _():
+        QB[...] = jnp.zeros_like(QB)
+
+    @pl.when(y == NY - 1)
+    def _():
+        QN[...] = jnp.zeros_like(QN)
 
     mine = resid.at[y, :, pl.ds(pl.multiple_of(h * half, 128), half)]
     keep = pltpu.make_async_copy(mine, X.at[r, x, a], loc.at[0])
@@ -65,7 +78,9 @@
     dec_in = pltpu.make_async_copy(dec.at[0], DW, loc.at[4])
     dec_in.start()
 
-    extra = jnp.where(jnp.logical_and(y > 0, y < NY - 1), 2, 1)
+    fire = pltpu.make_async_copy(blocks, BK, loc.at[7])
+    fire.start()
+    extra = jnp.where(y < NY - 1, 4, 0) + jnp.where(y > 0, 5, 0)
     pl.semaphore_wait(barrier, len(near) + extra)
 
     count = [0]
@@ -121,7 +136,8 @@
     bias_far = send(bias, BI.at[h], sibling)
     across = gathered(X, mine)
 
-    row = blocks[y]
+    fire.wait()
+    row = BK[y]
     column = x * NZ + z
     hits = [
         jnp.max((row == g * NX * NZ + column).astype(F32), axis=1, keepdims=True)
@@ -189,25 +205,66 @@
         for copy in copies:
             copy.wait_recv()
 
-    after = []
+    after, above, below = [], [], []
+    up_y = {"y": lax.rem(y + 1, NY)}
+    down_y = {"y": lax.rem(y + NY - 1, NY)}
+
+    def start_above(*copies):
+        above.extend(copies)
+
+        @pl.when(y < NY - 1)
+        def _():
+            for copy in copies:
+                copy.start()
+
+    def start_below(*copies):
+        below.extend(copies)
+
+        @pl.when(y > 0)
+        def _():
+            for copy in copies:
+                copy.start()
+
     for i, (d, rr) in enumerate(classes[:3]):
         landed(in1[d])
         B1[i] = summed1(lax.rem(x + d, NX)).astype(BF16)
+        start_above(made(B1.at[i], QB.at[i], {**up_y, **at_x(d)}))
         after.append(send(B1.at[i], Q1.at[i], at_x(d)))
         landed(in0[d])
         B0[i] = summed0(rr).astype(BF16)
         if d == 2:
-            after.append(send(B0.at[i, :, lo], Q0.at[i, :, lo], at_z(2)))
-            after.append(send(B0.at[i, :, hi], Q0.at[i, :, hi], at_z(-2)))
+            parts = ((lo, at_z(2)), (hi, at_z(-2)))
+            start_below(*[
+                made(B0.at[i, :, cols], QN.at[i, :, cols], {**down_y, **to})
+                for cols, to in parts
+            ])
+            after += [send(B0.at[i, :, cols], Q0.at[i, :, cols], to) for cols, to in parts]
         else:
-            after.append(send(B0.at[i], Q0.at[i], at_z(1 if d == 1 else -1)))
+            to = at_z(1 if d == 1 else -1)
+            start_below(made(B0.at[i], QN.at[i], {**down_y, **to}))
+            after.append(send(B0.at[i], Q0.at[i], to))
     landed(in1[0])
     own1 = summed1(x)
+    B1[3] = own1.astype(BF16)
+    start_above(made(B1.at[3], QB.at[3], up_y))
     landed(in0[0])
     own0 = summed0(r)
+    B0[3] = own0.astype(BF16)
+    start_below(made(B0.at[3], QN.at[3], down_y))
     landed(after)
-    for t, own, Q in ((0, own0, Q0), (1, own1, Q1)):
+
+    @pl.when(y > 0)
+    def _():
+        landed(above)
+
+    @pl.when(y < NY - 1)
+    def _():
+        landed(below)
+
+    for t, own, Q, QY in ((0, own0, Q0, QB), (1, own1, Q1, QN)):
         total = (own + Q[0].astype(F32)) + (Q[1].astype(F32) + Q[2].astype(F32))
+        total = total + (
+            (QY[0].astype(F32) + QY[1].astype(F32)) + (QY[2].astype(F32) + QY[3].astype(F32)))
         for aa in range(NA):
             two = total[2 * aa:2 * aa + 2, :]
             S2F[aa, t] = two
@@ -219,36 +276,10 @@
     for copy in last:
         copy.wait_recv()
     sums = S2F[a] + R2[0].astype(F32) + R2[1].astype(F32) + R2[2].astype(F32)
-    YO[...] = sums[0]
-    YA[...] = sums[1]
-
-    up_y = made(YA, YB, {"y": lax.rem(y + 1, NY)})
-    down_y = made(YO, YN, {"y": lax.rem(y + NY - 1, NY)})
-
-    @pl.when(y < NY - 1)
-    def _():
-        up_y.start()
-
-    @pl.when(y > 0)
-    def _():
-        down_y.start()
-        up_y.wait_recv()
-
-    @pl.when(y == 0)
-    def _():
-        YB[...] = jnp.zeros_like(YB)
-
-    @pl.when(y < NY - 1)
-    def _():
-        down_y.wait_recv()
-
-    @pl.when(y == NY - 1)
-    def _():
-        YN[...] = jnp.zeros_like(YN)
 
     tgt.wait()
-    err_own = (sums[0] + YB[...] - TG[0].astype(F32)).astype(BF16)
-    err_next = (YN[...] + sums[1] - TG[1].astype(F32)).astype(BF16)
+    err_own = (sums[0] - TG[0].astype(F32)).astype(BF16)
+    err_next = (sums[1] - TG[1].astype(F32)).astype(BF16)
     err_out[0] = err_own
     E[r, x, a, 0] = err_own
     E[r, x, a, 1] = err_next
@@ -261,20 +292,23 @@
 
     for copy in gathered(E, E.at[r, x, a]):
         copy.wait_recv()
-    grad = None
     for t in range(2):
         for rr in range(4):
-            EM[pl.ds(rr * 32, 32), :] = E[rr, :, :, t].reshape(32, half)
-        term = lax.dot_general(
-            EM[...], DW[t].reshape(2 * width, half), (((1,), (1,)), ((), ())),
-            preferred_element_type=F32)
-        grad = term if grad is None else grad + term
-    GP[0] = grad[:, :width]
-    GP[1] = grad[:, width:]
-    back = send(GP.at[other], GR, sibling)
-
+            EM[t, pl.ds(rr * 32, 32), :] = E[rr, :, :, t].reshape(32, half)
+
+    def latent_grad(g):
+        terms = [
+            lax.dot_general(
+                EM[t], DW[t, g], (((1,), (1,)), ((), ())), preferred_element_type=F32)
+            for t in range(2)
+        ]
+        return terms[0] + terms[1]
+
+    GP[...] = latent_grad(other)
+    back = send(GP, GR, sibling)
+    grad_own = latent_grad(h)
     back.wait_recv()
-    grad_pre = (GP[h] + GR[...]) * gate_own
+    grad_pre = (grad_own + GR[...]) * gate_own
     bias_out[...] = jnp.sum(grad_pre, axis=0, keepdims=True)
     low_out[...] = grad_pre.astype(BF16)
     for copy in started:
@@ -282,11 +316,13 @@
 
     @pl.when(y < NY - 1)
     def _():
-        up_y.wait_send()
+        for copy in above:
+            copy.wait_send()
 
     @pl.when(y > 0)
     def _():
-        down_y.wait_send()
+        for copy in below:
+            copy.wait_send()
 
     out_a.wait()
     out_b.wait()
@@ -299,6 +335,9 @@
     hbm = pl.BlockSpec(memory_space=pltpu.HBM)
     vmem = pl.BlockSpec(memory_space=pltpu.VMEM)
     V = pltpu.VMEM
+    resid, target, enc, bias, dec, blocks = (
+        pltpu.with_memory_space_constraint(v, pltpu.HBM)
+        for v in (resid, target, enc, bias, dec, blocks))
     x_all, low, bias_grad, errors = pl.pallas_call(
         body,
         out_shape=(
@@ -307,7 +346,7 @@
             jax.ShapeDtypeStruct((1, width), F32),
             jax.ShapeDtypeStruct((1, 2, half), BF16),
         ),
-        in_specs=[hbm] * 5 + [vmem],
+        in_specs=[hbm] * 6,
         out_specs=(vmem,) * 4,
         scratch_shapes=[
             V((4, NX, NA, 2, half), BF16),
@@ -324,21 +363,20 @@
             V((4, NX, 8, half), BF16),
             V((3, 4, 8, half), BF16),
             V((3, NX, 8, half), BF16),
-            V((3, 8, half), BF16),
-            V((3, 8, half), BF16),
+            V((4, 8, half), BF16),
+            V((4, 8, half), BF16),
             V((3, 8, half), BF16),
             V((3, 8, half), BF16),
             V((NA, 2, 2, half), BF16),
             V((NA, 2, 2, half), F32),
             V((3, 2, 2, half), BF16),
-            V((2, half), F32),
-            V((2, half), F32),
-            V((2, half), F32),
-            V((2, half), F32),
+            V((4, 8, half), BF16),
+            V((4, 8, half), BF16),
             V((4, NX, NA, 2, 2, half), BF16),
-            V((rows, half), BF16),
-            V((2, rows, width), F32),
+            V((2, rows, half), BF16),
             V((rows, width), F32),
+            V((rows, width), F32),
+            V(blocks.shape, jnp.int32),
             pltpu.SemaphoreType.DMA((8,)),
             pltpu.SemaphoreType.DMA((SENDS,)),
             pltpu.SemaphoreType.DMA((SENDS,)),

time: 75.2 us -> 71.6 us (0.952)
  local copies, waits for them, and re-layouts: 3.03 us -> 0 us
    unnamed x8 -> x0, local copies, waits for them, and re-layouts: 3.03 us -> none
where the time goes in v5:
time: 71.6 us; the launch traced here: 71.5 us
  Pallas kernels  70.8 us (99%)
    pallas_call x1, Pallas kernels, on_device(): pl.pallas_call(body, out_shape=(jax.ShapeDtypeStruct((2, half, rows), BF1...  69.1 us
    pallas_call x1, Pallas kernels, on_device(): pl.pallas_call(weight_gradient, out_shape=(jax.ShapeDtypeStruct((1, 2 * h...  1.78 us

profile of v5, /device:TPU:1, one launch (start us, length us, event | category | flops | bytes accessed | tf_op | source)
XLA Modules:
  0.0 71.5 jit_solution(13893796694617226173)
XLA Ops:
  0.6 69.1 %step.1 = (bf16[2,1792,128]{2,1,0:T(8,128)(2,1)S(1)}, bf16[128,128]{1,0:T(8,128)(2,1)S(1)}, f32[1,128]{1,0:T(1,128)S(1)}, bf16[1,2,1792]{2,1,0:T(2,128)(2,1)S(1)}) custom-call(bf16[4,2,3584]{2,1,0:T(2,128)(2,1)} %resid.1, bf16[5,2,3584]{2,1,0:T(2,128)(2,1)} %target.1, bf16[1,3584,128]{2,1,0:T(8,128)(2,1)} %enc.1, f32[1,128]{1,0:T(1,128)} %bias.1, ...), custom_call_target="tpu_custom_call" | custom-call | tf_op jit(solution)/shard_map/step/pallas_call | solution.py:341
  69.7 1.8 %weights.1 = (bf16[1,3584,128]{2,1,0:T(8,128)(2,1)}, f32[1,128]{1,0:T(1,128)}, bf16[1,2,1792]{2,1,0:T(2,128)(2,1)}) custom-call(bf16[3584,128]{1,0:T(8,128)(2,1)S(1)} %bitcast.1, bf16[128,128]{1,0:T(8,128)(2,1)S(1)} %get-tuple-element.11.low, f32[1,128]{1,0:T(1,128)S(1)} %get-tuple-element.12.bias_in, bf16[1,2,1792]{2,1,0:T(2,128)(2,1)S(1)} %get-tuple-element.13.err_in), custom_call_target="tpu_custom_call" | custom-call | tf_op jit(solution)/shard_map/weights/pallas_call | solution.py:389

commit v6 on v5

--- a/solution.py
+++ b/solution.py
@@ -18,7 +18,7 @@
 def body(
     resid, target, enc, bias, dec, blocks,
     x_out, low_out, bias_out, err_out,
-    X, XO, XO_T, XS_T, WE, BI, DW, TG, PP, PR, S0, S1, R0, R1, B0, B1, Q0, Q1,
+    X, XO, XS_T, WE, BI, DW, TG, PP, PR, S0, S1, R0, R1, B0, B1, Q0, Q1,
     S2, S2F, R2, QN, QB, E, EM, GP, GR, BK, loc, ssem, rsem,
 ):
     y, h = lax.axis_index("y"), lax.axis_index("core")
@@ -129,6 +129,53 @@
             far[d].wait_recv()
             across += passed(d)[1]
         return across
+
+    def gathered_even(buf):
+        own = buf.at[r, x, a]
+        out = {d: send(own, own, at_z(d)) for d in (4, -4, 3, -3, 2, -2, 1, -1)}
+        sides = {}
+        rest = [out[1], out[-1]]
+
+        def to_sides(d):
+            rr, aa = slot(-d)
+            got = buf.at[rr, x, aa]
+            sides[d] = [send(got, got, at_x(dx)) for dx in (2, 1, 3)]
+
+        def to_next(d, ways):
+            rr, aa = slot(-d)
+            copies = []
+            for dx, copy in zip((2, 1, 3), sides[d]):
+                copy.wait_recv()
+                got = buf.at[rr, lax.rem(x + NX - dx, NX), aa]
+                copies += [send(got, got, at_z(way)) for way in ways]
+            return copies
+
+        to_sides(0)
+        for d in (2, -2):
+            out[d].wait_recv()
+            to_sides(d)
+        for d in (3, -3):
+            out[d].wait_recv()
+            to_sides(d)
+        far = {}
+        for d, steps in ((4, (4, 3, 2, 1)), (-4, (-3, -2, -1))):
+            out[d].wait_recv()
+            rr, aa = slot(-d)
+            got = buf.at[rr, x, aa]
+            for k in steps:
+                far[k + d] = send(got, got, at_z(k))
+        for d in (4, -4):
+            to_sides(d)
+        rest += to_next(0, (1, -1))
+        for d in (6, -6, 7, -7, 8):
+            far[d].wait_recv()
+            to_sides(d)
+        for d in (4, -4):
+            rest += to_next(d, (1,) if d > 0 else (-1,))
+        rest += [far[5], far[-5]]
+        for d in (2, -2, 3, -3, 6, -6, 7, -7, 8):
+            rest += sides[d]
+        return rest
 
     enc_far = send(
         enc.at[0, pl.ds(pl.multiple_of(other * half, 128), half), :],
@@ -190,8 +237,8 @@
                     for i, dx in enumerate((2, 1, 3))
                 ]
     for n in range(0, half, step):
-        XO_T[n:n + step, :] = XO[:, n:n + step].T
-    rows_far = send(XO_T, XS_T, sibling)
+        x_out[h, n:n + step, :] = XO[:, n:n + step].T
+    rows_far = send(x_out.at[h], XS_T, sibling)
 
     def summed1(xx):
         return (S1[r, xx].astype(F32) + R1[0, xx].astype(F32)) + (
@@ -273,6 +320,9 @@
         send(S2.at[lax.rem(a + d, NA)], R2.at[i], at_z(4 * d if d < 3 else -4))
         for i, d in enumerate((2, 1, 3))
     ]
+    rows_far.wait_recv()
+    out_b = pltpu.make_async_copy(XS_T, x_out.at[other], loc.at[5])
+    out_b.start()
     for copy in last:
         copy.wait_recv()
     sums = S2F[a] + R2[0].astype(F32) + R2[1].astype(F32) + R2[2].astype(F32)
@@ -284,13 +334,7 @@
     E[r, x, a, 0] = err_own
     E[r, x, a, 1] = err_next
 
-    rows_far.wait_recv()
-    out_a = pltpu.make_async_copy(XO_T, x_out.at[h], loc.at[5])
-    out_b = pltpu.make_async_copy(XS_T, x_out.at[other], loc.at[6])
-    out_a.start()
-    out_b.start()
-
-    for copy in gathered(E, E.at[r, x, a]):
+    for copy in gathered_even(E):
         copy.wait_recv()
     for t in range(2):
         for rr in range(4):
@@ -324,7 +368,6 @@
         for copy in below:
             copy.wait_send()
 
-    out_a.wait()
     out_b.wait()
 
 
@@ -351,7 +394,6 @@
         scratch_shapes=[
             V((4, NX, NA, 2, half), BF16),
             V((rows, half), BF16),
-            V((half, rows), BF16),
             V((half, rows), BF16),
             V((half, 2 * width), BF16),
             V((2, 1, width), F32),

time: 71.6 us -> 70.5 us (0.985)
  Pallas kernels: 70.8 us -> 69.7 us
    pallas_call x1, Pallas kernels: 69.1 us -> 67.9 us  [on_device(): pl.pallas_call(body, out_shape=(jax.ShapeDtypeStruct((2, half, rows), BF1...]
where the time goes in v6:
time: 70.5 us; the launch traced here: 70.3 us
  Pallas kernels  69.7 us (99%)
    pallas_call x1, Pallas kernels, on_device(): pl.pallas_call(body, out_shape=(jax.ShapeDtypeStruct((2, half, rows), BF1...  67.9 us
    pallas_call x1, Pallas kernels, on_device(): pl.pallas_call(weight_gradient, out_shape=(jax.ShapeDtypeStruct((1, 2 * h...  1.78 us

profile of v6, /device:TPU:1, one launch (start us, length us, event | category | flops | bytes accessed | tf_op | source)
XLA Modules:
  0.0 70.3 jit_solution(4284472140374190204)
XLA Ops:
  0.6 67.9 %step.1 = (bf16[2,1792,128]{2,1,0:T(8,128)(2,1)S(1)}, bf16[128,128]{1,0:T(8,128)(2,1)S(1)}, f32[1,128]{1,0:T(1,128)S(1)}, bf16[1,2,1792]{2,1,0:T(2,128)(2,1)S(1)}) custom-call(bf16[4,2,3584]{2,1,0:T(2,128)(2,1)} %resid.1, bf16[5,2,3584]{2,1,0:T(2,128)(2,1)} %target.1, bf16[1,3584,128]{2,1,0:T(8,128)(2,1)} %enc.1, f32[1,128]{1,0:T(1,128)} %bias.1, ...), custom_call_target="tpu_custom_call" | custom-call | tf_op jit(solution)/shard_map/step/pallas_call | solution.py:384
  68.6 1.8 %weights.1 = (bf16[1,3584,128]{2,1,0:T(8,128)(2,1)}, f32[1,128]{1,0:T(1,128)}, bf16[1,2,1792]{2,1,0:T(2,128)(2,1)}) custom-call(bf16[3584,128]{1,0:T(8,128)(2,1)S(1)} %bitcast.1, bf16[128,128]{1,0:T(8,128)(2,1)S(1)} %get-tuple-element.11.low, f32[1,128]{1,0:T(1,128)S(1)} %get-tuple-element.12.bias_in, bf16[1,2,1792]{2,1,0:T(2,128)(2,1)S(1)} %get-tuple-element.13.err_in), custom_call_target="tpu_custom_call" | custom-call | tf_op jit(solution)/shard_map/weights/pallas_call | solution.py:431

commit v7 on v6

--- a/solution.py
+++ b/solution.py
@@ -106,33 +106,6 @@
     def gathered(buf, src):
         own = buf.at[r, x, a]
         out = {d: send(src, own, at_z(d)) for d in (4, -4, 3, -3, 2, -2, 1, -1)}
-        across = [send(src, own, at_x(d)) for d in (2, 1, 3)]
-
-        def passed(d):
-            rr, aa = slot(-d)
-            got = buf.at[rr, x, aa]
-            return got, [send(got, got, at_x(dx)) for dx in (2, 1, 3)]
-
-        for d in (1, -1, 2, -2, 3, -3):
-            out[d].wait_recv()
-            across += passed(d)[1]
-        far = {}
-        for d, steps in ((4, (4, 3, 2, 1)), (-4, (-3, -2, -1))):
-            out[d].wait_recv()
-            rr, aa = slot(-d)
-            got = buf.at[rr, x, aa]
-            for k in steps:
-                far[k + d] = send(got, got, at_z(k))
-        for d in (4, -4):
-            across += passed(d)[1]
-        for d in (5, -5, 6, -6, 7, -7, 8):
-            far[d].wait_recv()
-            across += passed(d)[1]
-        return across
-
-    def gathered_even(buf):
-        own = buf.at[r, x, a]
-        out = {d: send(own, own, at_z(d)) for d in (4, -4, 3, -3, 2, -2, 1, -1)}
         sides = {}
         rest = [out[1], out[-1]]
 
@@ -150,7 +123,7 @@
                 copies += [send(got, got, at_z(way)) for way in ways]
             return copies
 
-        to_sides(0)
+        sides[0] = [send(src, own, at_x(dx)) for dx in (2, 1, 3)]
         for d in (2, -2):
             out[d].wait_recv()
             to_sides(d)
@@ -334,7 +307,7 @@
     E[r, x, a, 0] = err_own
     E[r, x, a, 1] = err_next
 
-    for copy in gathered_even(E):
+    for copy in gathered(E, E.at[r, x, a]):
         copy.wait_recv()
     for t in range(2):
         for rr in range(4):

time: 70.5 us -> 70.5 us (level)
  no operation moved by 1% of the time
where the time goes in v7:
time: 70.5 us; the launch traced here: 70.4 us
  Pallas kernels  69.7 us (99%)
    pallas_call x1, Pallas kernels, on_device(): pl.pallas_call(body, out_shape=(jax.ShapeDtypeStruct((2, half, rows), BF1...  67.9 us
    pallas_call x1, Pallas kernels, on_device(): pl.pallas_call(weight_gradient, out_shape=(jax.ShapeDtypeStruct((1, 2 * h...  1.78 us

profile of v7, /device:TPU:1, one launch (start us, length us, event | category | flops | bytes accessed | tf_op | source)
XLA Modules:
  0.0 70.4 jit_solution(1455460522005885528)
XLA Ops:
  0.6 67.9 %step.1 = (bf16[2,1792,128]{2,1,0:T(8,128)(2,1)S(1)}, bf16[128,128]{1,0:T(8,128)(2,1)S(1)}, f32[1,128]{1,0:T(1,128)S(1)}, bf16[1,2,1792]{2,1,0:T(2,128)(2,1)S(1)}) custom-call(bf16[4,2,3584]{2,1,0:T(2,128)(2,1)} %resid.1, bf16[5,2,3584]{2,1,0:T(2,128)(2,1)} %target.1, bf16[1,3584,128]{2,1,0:T(8,128)(2,1)} %enc.1, f32[1,128]{1,0:T(1,128)} %bias.1, ...), custom_call_target="tpu_custom_call" | custom-call | tf_op jit(solution)/shard_map/step/pallas_call | solution.py:357
  68.6 1.8 %weights.1 = (bf16[1,3584,128]{2,1,0:T(8,128)(2,1)}, f32[1,128]{1,0:T(1,128)}, bf16[1,2,1792]{2,1,0:T(2,128)(2,1)}) custom-call(bf16[3584,128]{1,0:T(8,128)(2,1)S(1)} %bitcast.1, bf16[128,128]{1,0:T(8,128)(2,1)S(1)} %get-tuple-element.11.low, f32[1,128]{1,0:T(1,128)S(1)} %get-tuple-element.12.bias_in, bf16[1,2,1792]{2,1,0:T(2,128)(2,1)S(1)} %get-tuple-element.13.err_in), custom_call_target="tpu_custom_call" | custom-call | tf_op jit(solution)/shard_map/weights/pallas_call | solution.py:404
